TPU v7x, 128 devices: a whole 4x4x4 slice. The times are simulated.
128 devices in a mesh: section: 2 (over core), dp: 16 (over y, x), tensor: 4 (over z).
Axes of the slice: x: 4, y: 4, z: 4, core: 2. Of those that a mesh axis runs over, the one named last changes fastest.
Arguments:
- layer_input: bfloat16 [2, 4096, 2, 4096], P('section', 'dp', None, 'tensor'), may hold values from -60 to 60
- norm_gain: float32 [2, 4096], P('section'), may hold values from 0.5 to 1.5
- upstream_grad: bfloat16 [2, 4096, 2, 4096], P('section', 'dp', None, 'tensor'), may hold values from -80 to 80
- saved_queries: bfloat16 [2, 4096, 2, 2048], P('section', 'dp', None, 'tensor'), may hold values from -150 to 150
- saved_keys: bfloat16 [2, 4096, 2, 1024], P('section', 'dp', None, 'tensor'), may hold values from -5 to 5
- saved_values: bfloat16 [2, 4096, 2, 1024], P('section', 'dp', None, 'tensor'), may hold values from -6 to 6
- segment_ids: int32 [2, 2, 4096], P('section', None, 'dp'), may hold values from 0 to 63, never falling along the last dimension, each value on 1 to 128 neighbouring positions
- batch_order: int32 [2, 16, 2], P('section', 'dp'), may hold values from 0 to 1, each once within a row
- qkv_weight: bfloat16 [2, 4096, 4096], P('section', None, 'tensor'), may hold values from -0.09375 to 0.09375
- out_weight: bfloat16 [2, 2048, 4096], P('section', 'tensor'), may hold values from -0.125 to 0.125
Outputs:
- passed_grad: bfloat16 [2, 4096, 2, 4096], P('section', 'dp', None, 'tensor')
- qkv_grad: float32 [2, 4096, 4096], P('section', 'dp', 'tensor')
- out_grad: float32 [2, 2048, 4096], P('section', 'tensor', 'dp')
- gain_grad: float32 [2, 4096], P('section', 'tensor')
All inputs are finite; a program needn't handle non-finite values.
Results may differ from a plain program's by a relative error of at most 0.0058.
The roundings to bfloat16 on the way count: a program that leaves them out, or rounds other values in their place, can miss the bound.
Values may be sent and summed in bfloat16 or wider, within the bound.
A program may use at most 192 MiB of HBM per device.

v0:
```python
import math

import jax
import jax.numpy as jnp
from jax import lax
from jax.sharding import PartitionSpec as P

HD = 128
KV = 8
HEADS = 16


EPS = 1e-05


def from_behind(value, axis, steps):
    count = lax.axis_size(axis)
    first, last = (max(0, -steps), min(count, count - steps))
    return lax.ppermute(value, axis, [(source, source + steps) for source in range(first, last)])


def attention_back(queries, saved_keys, saved_values, visible, attn_grad):
    score_scale = 1.0 / math.sqrt(HD)
    visible_full = visible[:, None, None, :, :]
    scores = (
        jnp.einsum("ibkgh,jbkh->bkgij", queries, saved_keys, preferred_element_type=jnp.float32)
        * score_scale
    )
    scores = jnp.where(visible_full, scores, -1e30)
    row_max = jnp.max(scores, axis=-1, keepdims=True)
    exp_scores = jnp.where(visible_full, jnp.exp(scores - row_max), 0.0)
    attn_probs = exp_scores / jnp.sum(exp_scores, axis=-1, keepdims=True)
    probs_bf16 = attn_probs.astype(jnp.bfloat16)
    attn_out = jnp.einsum(
        "bkgij,jbkh->ibkgh", probs_bf16, saved_values, preferred_element_type=jnp.float32
    ).astype(jnp.bfloat16)
    probs_grad = jnp.einsum(
        "ibkgh,jbkh->bkgij", attn_grad, saved_values, preferred_element_type=jnp.float32
    )
    row_dot = jnp.sum(attn_probs * probs_grad, axis=-1, keepdims=True)
    score_grad = (attn_probs * (probs_grad - row_dot) * score_scale).astype(jnp.bfloat16)
    query_grad = jnp.einsum(
        "bkgij,jbkh->ibkgh", score_grad, saved_keys, preferred_element_type=jnp.float32
    )
    key_grad = jnp.einsum(
        "bkgij,ibkgh->jbkh", score_grad, queries, preferred_element_type=jnp.float32
    )
    value_grad = jnp.einsum(
        "bkgij,ibkgh->jbkh", probs_bf16, attn_grad, preferred_element_type=jnp.float32
    )
    qkv_grads = jnp.concatenate(
        [query_grad, key_grad[..., None, :], value_grad[..., None, :]], axis=-2
    )
    return (attn_out, qkv_grads.astype(jnp.bfloat16))


def layer_back(
    inputs,
    upstream,
    queries,
    keys_local,
    values_local,
    segment_rows,
    gain_vec,
    weights_qkv,
    weights_out,
):
    seq_len, batch_count, local_width = inputs.shape
    inputs_full, upstream_full = (
        lax.all_gather(inputs, "tensor", axis=2, tiled=True),
        lax.all_gather(upstream, "tensor", axis=2, tiled=True),
    )
    model_width = inputs_full.shape[2]
    widened = inputs_full.astype(jnp.float32)
    root_mean = jnp.sqrt(jnp.mean(widened * widened, axis=-1, keepdims=True) + EPS)
    unit_rows = widened / root_mean
    normed_full = (unit_rows * gain_vec).astype(jnp.bfloat16)
    attn_grad = jnp.einsum(
        "ibd,cd->ibc", upstream_full, weights_out, preferred_element_type=jnp.float32
    ).astype(jnp.bfloat16)
    kv_local = keys_local.shape[-1] // HD
    group_size = HEADS // KV
    query_shape = (seq_len, batch_count, kv_local, group_size, HD)
    value_shape = (seq_len, batch_count, kv_local, HD)
    positions = jnp.arange(seq_len)
    causal = positions[None, :] <= positions[:, None]
    visible = (segment_rows[:, :, None] == segment_rows[:, None, :]) & causal[None]
    attn_out, qkv_grads = attention_back(
        queries.reshape(query_shape),
        keys_local.reshape(value_shape),
        values_local.reshape(value_shape),
        visible,
        attn_grad.reshape(query_shape),
    )
    attn_out = attn_out.reshape(seq_len, batch_count, -1)
    qkv_grads = qkv_grads.reshape(seq_len, batch_count, -1)
    grad_terms = jnp.einsum(
        "ibc,dc->ibd", qkv_grads, weights_qkv, preferred_element_type=jnp.float32
    )
    normed_grad = lax.psum_scatter(grad_terms, "tensor", scatter_dimension=2, tiled=True)
    first_col = lax.axis_index("tensor") * local_width
    unit_local = lax.dynamic_slice_in_dim(unit_rows, first_col, local_width, 2)
    gain_local = lax.dynamic_slice_in_dim(gain_vec, first_col, local_width, 0)
    scaled = normed_grad * gain_local
    row_part = jnp.sum(scaled * unit_local, axis=-1, keepdims=True)
    row_total = lax.psum(row_part, "tensor")
    through = (
        upstream.astype(jnp.float32) + (scaled - unit_local * (row_total / model_width)) / root_mean
    )
    gain_part = jnp.sum(normed_grad * unit_local, axis=(0, 1))
    return (
        through.astype(jnp.bfloat16),
        gain_part,
        normed_full,
        upstream_full,
        attn_out,
        qkv_grads,
    )


def shards(
    layer_input,
    norm_gain,
    upstream_grad,
    saved_queries,
    saved_keys,
    saved_values,
    segment_ids,
    batch_order,
    qkv_weight,
    out_weight,
):
    inputs = layer_input[0]
    upstream = upstream_grad[0]
    gain_vec = norm_gain[0]
    queries = saved_queries[0]
    keys_local = saved_keys[0]
    values_local = saved_values[0]
    id_rows = segment_ids[0]
    order_row = batch_order[0, 0]
    weights_qkv = qkv_weight[0]
    weights_out = out_weight[0]
    through, gain_part, normed_full, upstream_full, attn_out, qkv_grads = layer_back(
        inputs,
        upstream,
        queries,
        keys_local,
        values_local,
        id_rows,
        gain_vec,
        weights_qkv,
        weights_out,
    )
    ordered = jnp.take(through, order_row, axis=1)
    passed = from_behind(ordered, "section", -1)
    replicas = lax.axis_size("dp")
    qkv_total = jnp.einsum(
        "ibd,ibc->dc", normed_full, qkv_grads, preferred_element_type=jnp.float32
    )
    out_total = jnp.einsum(
        "ibc,ibd->cd", attn_out, upstream_full, preferred_element_type=jnp.float32
    )
    qkv_grad = lax.psum_scatter(qkv_total, "dp", scatter_dimension=0, tiled=True) / replicas
    out_grad = lax.psum_scatter(out_total, "dp", scatter_dimension=1, tiled=True) / replicas
    gain_grad = lax.psum(gain_part, "dp") / replicas
    return (passed[None], qkv_grad[None], out_grad[None], gain_grad[None])


def solution(mesh):
    placed = (
        P("section", "dp", None, "tensor"),
        P("section", None),
        P("section", "dp", None, "tensor"),
        P("section", "dp", None, "tensor"),
        P("section", "dp", None, "tensor"),
        P("section", "dp", None, "tensor"),
        P("section", None, "dp"),
        P("section", "dp", None),
        P("section", None, "tensor"),
        P("section", "tensor", None),
    )
    return jax.shard_map(
        shards,
        mesh=mesh,
        in_specs=placed,
        out_specs=(
            P("section", "dp", None, "tensor"),
            P("section", "dp", "tensor"),
            P("section", "tensor", "dp"),
            P("section", "tensor"),
        ),
        check_vma=False,
    )
```

profile of v0, /device:TPU:0, one launch (start us, length us, event | category | flops | bytes accessed | tf_op | source)
XLA Modules:
  0.0 406.4 jit_solution(5581653968323635845)
XLA Ops:
  7.2 2.5 copy.14
  9.9 1.2 copy.27
  12.2 0.5 copy.54
  12.9 2.4 fusion.35
  15.3 45.9 %all-gather.5.cloned.1.call-done = bf16[1,256,2,4096]{3,1,2,0:T(8,128)(2,1)} async-done(((bf16[1,256,2,1024]{3,1,2,0:T(8,128)(2,1)}), bf16[1,256,2,4096]{3,1,2,0:T(8,128)(2,1)}) %all-gather.5.cloned.1.call-update) | async-done | bytes 4194320 | tf_op jit(solution)/shard_map/all_gather | solution.py:71
  61.2 5.8 %fusion.15 = bf16[256,2,512]{2,0,1:T(8,128)(2,1)S(1)} fusion(bf16[1,512,4096]{2,1,0:T(8,128)(2,1)} %param.19, bf16[1,256,2,4096]{3,1,2,0:T(8,128)(2,1)} %all-gather.5.cloned.1.call-done), kind=kOutput, calls=%fused_computation.30 | convolution fusion | flops 2147745792 | bytes 8912896 | tf_op jit(solution)/shard_map/ibd,cd->ibc/dot_general | solution.py:78
  67.2 0.5 fusion.36
  67.7 3.7 convolution_bitcast_fusion.4
  71.4 3.5 convolution_bitcast_fusion.2
  74.9 2.3 convolution_bitcast_fusion.3
  77.4 10.3 %fusion.3 = f32[256,2,4096]{2,0,1:T(8,128)} fusion(bf16[256,2,1024]{0,2,1:T(8,128)(2,1)S(1)} %bitcast.116, bf16[1,4096,1024]{2,1,0:T(8,128)(2,1)} %param.18), kind=kOutput, calls=%fused_computation.7 | convolution fusion | flops 4294967296 | bytes 17825792 | tf_op jit(solution)/shard_map/ibc,dc->ibd/dot_general | solution.py:97
  87.9 2.1 convolution_convert_fusion
  90.0 0.8 copy-done.2
  90.8 5.6 %convolution_bitcast_fusion.1 = f32[512,4096]{1,0:T(8,128)} fusion(bf16[256,2,512]{0,2,1:T(8,128)(2,1)S(1)} %bitcast.121, bf16[1,256,2,4096]{3,1,2,0:T(8,128)(2,1)S(1)} %copy-done.2), kind=kOutput, calls=%fused_computation.10 | convolution fusion | flops 2147483648 | bytes 13107200 | tf_op jit(solution)/shard_map/ibc,ibd->cd/dot_general | solution.py:160
  96.4 15.7 %all-gather.7.cloned.1.call-done = bf16[1,256,2,4096]{3,1,2,0:T(8,128)(2,1)} async-done(((bf16[1,256,2,1024]{3,1,2,0:T(8,128)(2,1)}), bf16[1,256,2,4096]{3,1,2,0:T(8,128)(2,1)}) %all-gather.7.cloned.1.call-update) | async-done | bytes 4194320 | tf_op jit(solution)/shard_map/all_gather | solution.py:70
  112.1 3.2 fusion.2
  115.5 8.6 %convolution_bitcast_fusion = f32[4096,1024]{1,0:T(8,128)} fusion(bf16[256,2,1024]{0,2,1:T(8,128)(2,1)S(1)} %bitcast.117, f32[4096]{0:T(1024)S(1)} %bitcast.129, bf16[1,256,2,4096]{3,1,2,0:T(8,128)(2,1)S(1)} %copy-done, f32[256,2]{0,1:T(2,128)S(1)} %add_sqrt_fusion), kind=kOutput, calls=%fused_computation.5 | convolution fusion | flops 4303355904 | bytes 22038528 | tf_op jit(solution)/shard_map/ibd,ibc->dc/dot_general | solution.py:157
  124.2 0.6 copy-done.11
  124.9 6.7 %convert_divide_fusion = f32[256,2,4096]{2,0,1:T(8,128)} fusion(bf16[1,256,2,4096]{3,1,2,0:T(8,128)(2,1)} %all-gather.7.cloned.1.call-done, f32[256,2]{0,1:T(2,128)S(1)} %add_sqrt_fusion), kind=kLoop, calls=%fused_computation.3 | loop fusion | flops 4194304 | bytes 12584960 | tf_op jit(solution)/shard_map/div | solution.py:76
  131.6 63.9 %reduce-scatter.4.cloned.1.call-done = f32[256,2,1024]{2,0,1:T(8,128)} async-done(((f32[256,2,4096]{2,0,1:T(8,128)}), f32[256,2,1024]{2,0,1:T(8,128)}) %reduce-scatter.4.cloned.1.call-update) | async-done | bytes 2097168 | tf_op jit(solution)/shard_map/reduce_scatter | solution.py:100
  195.5 2.9 multiply_reduce_fusion
  198.4 8.5 %psum.14 = f32[256,2,1]{0,1,2:T(2,128)S(1)} all-reduce(f32[256,2,1]{0,1,2:T(2,128)S(1)} %bitcast.126), channel_id=1, replica_groups=mesh['section'=2,'dp'=16,'tensor'=4] {'tensor'}, use_global_device_ids=true, to_apply=%region_6.7 | all-reduce | flops 512 | bytes 4096 | tf_op jit(solution)/shard_map/psum | solution.py:106
  206.9 2.7 fusion.10
  209.6 0.6 gather_fusion
  210.4 1.3 collective-permute-start
  211.7 40.9 %psum.15 = f32[1024]{0:T(1024)S(1)} all-reduce(f32[1024]{0:T(1024)S(1)} %get-tuple-element.8), channel_id=1, replica_groups=mesh['section'=2,'dp'=16,'tensor'=4] {'dp'}, use_global_device_ids=true, to_apply=%region_10.11 | all-reduce | flops 1024 | bytes 8192 | tf_op jit(solution)/shard_map/psum | solution.py:165
  252.6 0.6 broadcast_multiply_fusion
  253.2 31.0 %reduce-scatter.8.cloned.1.call-done = f32[512,256]{1,0:T(8,128)} async-done(((f32[512,4096]{1,0:T(8,128)}), f32[512,256]{1,0:T(8,128)}) %reduce-scatter.8.cloned.1.call-update) | async-done | bytes 524304 | tf_op jit(solution)/shard_map/reduce_scatter | solution.py:164
  284.2 1.9 multiply_bitcast_fusion.1
  286.1 2.0 copy.32
  288.1 109.4 %reduce-scatter.6.cloned.1.call-done = f32[256,1024]{1,0:T(8,128)} async-done(((f32[4096,1024]{1,0:T(8,128)}), f32[256,1024]{1,0:T(8,128)}) %reduce-scatter.6.cloned.1.call-update) | async-done | bytes 1048592 | tf_op jit(solution)/shard_map/reduce_scatter | solution.py:163
  397.6 2.3 multiply_bitcast_fusion
  (48 shorter events, 2.3 us)
Async XLA Ops:
  7.2 2.7 copy-start.3
  7.2 54.0 %all-gather.5.cloned.1.call-start = ((), (), s32[]{:S(2)}) async-start(), calls=%async_computation.6 | async-start | bytes 5242880 | tf_op jit(solution)/shard_map/all_gather | solution.py:71
  9.8 1.4 copy-start.5
  9.8 1.8 copy-start.6
  9.8 102.3 %all-gather.7.cloned.1.call-start = ((), (), s32[]{:S(2)}) async-start(), calls=%async_computation.7 | async-start | bytes 5242880 | tf_op jit(solution)/shard_map/all_gather | solution.py:70
  11.1 1.0 copy-start.4
  11.1 1.6 copy-start.9
  11.1 184.3 %reduce-scatter.4.cloned.1.call-start = ((), (), s32[]{:S(2)}) async-start(), calls=%async_computation.3 | async-start | bytes 10485760 | tf_op jit(solution)/shard_map/reduce_scatter | solution.py:100
  11.6 3.7 copy-start.7
  74.9 2.3 copy-start.8
  87.7 196.5 %reduce-scatter.8.cloned.1.call-start = ((), (), s32[]{:S(2)}) async-start(), calls=%async_computation.5 | async-start | bytes 8912896 | tf_op jit(solution)/shard_map/reduce_scatter | solution.py:164
  87.9 2.9 copy-start.2
  96.3 19.0 %copy-start.10 = (f32[1,4096]{1,0:T(1,128)S(1)}, f32[1,4096]{1,0:T(1,128)}, u32[]{:S(2)}) copy-start(f32[1,4096]{1,0:T(1,128)} %param.11) | copy-start | bytes 49156
  96.4 301.2 %reduce-scatter.6.cloned.1.call-start = ((), (), s32[]{:S(2)}) async-start(), calls=%async_computation.4 | async-start | bytes 17825792 | tf_op jit(solution)/shard_map/reduce_scatter | solution.py:163
  112.1 3.4 copy-start
  124.2 0.7 copy-start.11
  195.5 11.4 %copy-start.1 = (f32[256,2,1024]{2,0,1:T(8,128)S(1)}, f32[256,2,1024]{2,0,1:T(8,128)}, u32[]{:S(2)}) copy-start(f32[256,2,1024]{2,0,1:T(8,128)} %reduce-scatter.4.cloned.1.call-done) | copy-start | bytes 6291460
  210.4 75.7 %collective-permute-start = (bf16[256,2,1024]{2,0,1:T(8,128)(2,1)S(1)}, bf16[256,2,1024]{2,0,1:T(8,128)(2,1)S(1)}, u32[]{:S(2)}, u32[]{:S(2)}) collective-permute-start(bf16[256,2,1024]{2,0,1:T(8,128)(2,1)S(1)} %select_bitcast_fusion), channel_id=1, source_target_pairs={{64,0},{65,1},{66,2},{67,3},{68,4},{69,5},{70,6},{71,7},{72,8},{73... | collective-permute-start | bytes 3145736 | tf_op jit(solution)/shard_map/ppermute | solution.py:19
Sparse Core Ops, SparseCore 0:
  10.2 50.9 all-gather.4
  63.4 48.6 all-gather.6
  114.6 80.8 reduce-scatter.3
  198.7 85.4 reduce-scatter.7
  287.5 110.0 reduce-scatter.5
where the time goes:
time: 407 us; the launch traced here: 406 us
  waiting for transfers between devices  266 us (65%)
  blocking collectives  49.5 us (12%)
  matrix products  44.8 us (11%)
  other arithmetic  20.8 us (5%)
  between operations  14 us (3%)
  local copies, waits for them, and re-layouts  9.73 us (2%)
    reduce_scatter x1, waiting for transfers between devices, shards(): lax.psum_scatter(qkv_total, 'dp', scatter_dimension=0, tiled=True)  109 us
    reduce_scatter x1, waiting for transfers between devices, layer_back(): lax.psum_scatter(grad_terms, 'tensor', scatter_dimension=2, tiled=True)  63.9 us
    all_gather x1, waiting for transfers between devices, layer_back(): lax.all_gather(upstream, 'tensor', axis=2, tiled=True)  45.9 us
    psum x1, blocking collectives, shards(): gain_grad = lax.psum(gain_part, 'dp') / replicas  40.9 us
    reduce_scatter x1, waiting for transfers between devices, shards(): lax.psum_scatter(out_total, 'dp', scatter_dimension=1, tiled=True)  31 us
    all_gather x1, waiting for transfers between devices, layer_back(): lax.all_gather(inputs, 'tensor', axis=2, tiled=True)  15.7 us
    dot_general x1, matrix products, layer_back(): jnp.einsum('ibc,dc->ibd', qkv_grads, weights_qkv, preferred_element_type=...  10.3 us
    dot_general x1, matrix products, shards(): jnp.einsum('ibd,ibc->dc', normed_full, qkv_grads, preferred_element_type=...  8.64 us
  transfers between devices with their start and end apart: 6, of which 5 were waited for; matrix products, arithmetic and copies ran while one was open for 17% of the time, Pallas kernels for 0%

commit v1 on v0

v1 whole, which is shorter than its diff:
```python
import math

import jax
import jax.numpy as jnp
from jax import lax
from jax.experimental import pallas as pl
from jax.experimental.pallas import tpu as pltpu
from jax.sharding import PartitionSpec as P

HD = 128
EPS = 1e-05
MESH = pl.DeviceIdType.MESH
F32 = jnp.float32
BF16 = jnp.bfloat16
SCALE = 1.0 / math.sqrt(HD)

NT = (((1,), (1,)), ((), ()))
NN = (((1,), (0,)), ((), ()))
TN = (((0,), (0,)), ((), ()))


def dot(a, b, dims):
    return lax.dot_general(a, b, dims, preferred_element_type=F32)


def rows_of(index, size):
    return pl.ds(pl.multiple_of(index * size, size), size)


def as_row(column):
    return jnp.broadcast_to(column, (256, 128)).T[0:8, :]


def as_column(row):
    return jnp.broadcast_to(row, (128, 256)).T


def kernel(
    up, inp, q, k, v, seg, gain, order, wq_hbm, wo_hbm,
    passed, qg, og, gg,
    upb, nm, wo, wq, probs, ao, aga, ag, qk,
    o_s, o_y1, o_y2, o_x, o_x1, o_x2,
    q_s, q_x1, q_x2, q_y, q_y1, q_y2,
    g_1, g_2, ssq, rowp, root, rtot, segc, gp, gz, gx, gy,
    lsem, ssem, rsem,
):
    sec = lax.axis_index("section")
    dp = lax.axis_index("dp")
    z = lax.axis_index("tensor")
    y = lax.div(dp, 4)
    x = lax.rem(dp, 4)

    z_to = [{"tensor": lax.rem(z + s, 4)} for s in range(4)]
    x_to = [{"dp": y * 4 + lax.rem(x + s, 4)} for s in range(4)]
    y_to = [{"dp": lax.rem(y + s, 4) * 4 + x} for s in range(4)]
    other = {"section": 1 - sec}

    counter = [0]
    sent = []

    def copy(src, dst, to, keep=True):
        index = counter[0]
        counter[0] += 1
        made = pltpu.make_async_remote_copy(
            src_ref=src,
            dst_ref=dst,
            send_sem=ssem.at[index],
            recv_sem=rsem.at[index],
            device_id=to,
            device_id_type=MESH,
        )
        if keep:
            sent.append(made)
        return made

    loads = [
        pltpu.make_async_copy(wo_hbm.at[:, pl.ds(1024 * b, 1024)], wo.at[b], lsem.at[b])
        for b in range(4)
    ]
    loads.append(pltpu.make_async_copy(wq_hbm, wq, lsem.at[4]))
    for one in loads:
        one.start()

    barrier = pltpu.get_barrier_semaphore()
    peers = z_to[1:] + x_to[1:] + y_to[1:] + [other]
    for peer in peers:
        pl.semaphore_signal(barrier, inc=1, device_id=peer, device_id_type=MESH)
    pl.semaphore_wait(barrier, len(peers))

    first, second = pl.ds(0, 256), pl.ds(256, 256)

    def gather_start(own, slots):
        made = {
            "ra": copy(own.at[first], slots[1].at[first], z_to[1]),
            "lb": copy(own.at[second], slots[2].at[second], z_to[3]),
            "rb": copy(own.at[second], slots[1].at[second], z_to[1]),
            "la": copy(own.at[first], slots[2].at[first], z_to[3]),
        }
        for name in ("ra", "lb", "rb", "la"):
            made[name].start()
        return made

    def gather_relay(made, slots):
        made["ra"].wait_recv()
        made["fa"] = copy(slots[1].at[first], slots[3].at[first], z_to[1])
        made["fa"].start()
        made["lb"].wait_recv()
        made["fb"] = copy(slots[2].at[second], slots[3].at[second], z_to[3])
        made["fb"].start()

    def add_rows(dst, src, count, step=32):
        @pl.loop(0, count // step)
        def _(i):
            part = rows_of(i, step)
            dst[part, :] = (dst[part, :].astype(F32) + src[part, :].astype(F32)).astype(BF16)

    def scatter(far, right, left, half, land, full, to, keep=True):
        return {
            "a": copy(far.at[pl.ds(0, half)], land.at[0], to[1], keep),
            "b": copy(far.at[pl.ds(half, half)], land.at[1], to[3], keep),
            "r": copy(right, full.at[0], to[1], keep),
            "l": copy(left, full.at[1], to[3], keep),
            "add_a": (right.at[pl.ds(0, half)], land.at[0], half),
            "add_b": (left.at[pl.ds(half, half)], land.at[1], half),
        }

    def scatter_start(made):
        made["a"].start()
        made["b"].start()

    def scatter_mid(made):
        made["a"].wait_recv()
        add_rows(*made["add_a"])
        made["r"].start()
        made["b"].wait_recv()
        add_rows(*made["add_b"])
        made["l"].start()

    def scatter_wait(made):
        made["r"].wait_recv()
        made["l"].wait_recv()

    up_slots = [up, upb.at[0], upb.at[1], upb.at[2]]
    nm_slots = [nm.at[0], nm.at[1], nm.at[2], nm.at[3]]
    offsets = (0, 3, 1, 2)

    up_made = gather_start(up, up_slots)

    for m in range(2):
        total = jnp.zeros((256, 1), F32)
        for c in range(4):
            wide = inp[pl.ds(256 * m, 256), pl.ds(256 * c, 256)].astype(F32)
            total += jnp.sum(wide * wide, axis=-1, keepdims=True)
        ssq[0, :, pl.ds(256 * m, 256)] = as_row(total)
    ssq_made = [copy(ssq.at[0], ssq.at[s], z_to[s]) for s in (1, 2, 3)]
    for one in ssq_made:
        one.start()

    for m in range(2):
        ids = seg[pl.ds(m, 1), :].astype(F32)
        segc[pl.ds(256 * m, 256), :] = jnp.broadcast_to(ids, (256, 256)).T

    @pl.loop(0, 8)
    def _(i):
        m = lax.div(i, 4)
        head = lax.rem(i, 4)
        rows = rows_of(m, 256)
        lanes = rows_of(lax.div(head, 2), 128)
        scores = dot(q[rows, rows_of(head, 128)], k[rows, lanes], NT) * SCALE
        low = lax.broadcasted_iota(jnp.int32, (256, 256), 0)
        high = lax.broadcasted_iota(jnp.int32, (256, 256), 1)
        ids = seg[pl.ds(m, 1), :].astype(F32)
        visible = (segc[rows, :] == ids) & (high <= low)
        scores = jnp.where(visible, scores, -1e30)
        top = jnp.max(scores, axis=-1, keepdims=True)
        shifted = jnp.where(visible, jnp.exp(scores - top), 0.0)
        weights = shifted / jnp.sum(shifted, axis=-1, keepdims=True)
        probs[i] = weights
        ao[rows, rows_of(head, 128)] = dot(weights.astype(BF16), v[rows, lanes], NN).astype(BF16)

    for one in loads[:4]:
        one.wait()

    def take_upstream(slot):
        block = lax.rem(z + offsets[slot], 4)
        ref = up_slots[slot]

        @pl.loop(0, 2)
        def _(m):
            rows = rows_of(m, 256)
            term = dot(ref[rows, :], wo[block], NT)
            if slot == 0:
                aga[rows, :] = term
            else:
                aga[rows, :] += term

    def out_terms(slot):
        block = lax.rem(z + offsets[slot], 4)
        ref = up_slots[slot]

        @pl.loop(0, 4)
        def _(j):
            lanes = rows_of(j, 256)
            o_s[block, :, lanes] = dot(ao[...], ref[:, lanes], TN).astype(BF16)

    take_upstream(0)
    out_terms(0)
    gather_relay(up_made, up_slots)

    for one in ssq_made:
        one.wait_recv()
    gain_own = gain[:, pl.ds(pl.multiple_of(z * 1024, 1024), 1024)]
    for m in range(2):
        lanes = pl.ds(256 * m, 256)
        total = ssq[0, :, lanes] + ssq[1, :, lanes] + ssq[2, :, lanes] + ssq[3, :, lanes]
        root[lanes, :] = as_column(jnp.sqrt(total * (1.0 / 4096) + EPS)[0:1, :])

    @pl.loop(0, 16)
    def _(i):
        rows = rows_of(i, 32)
        unit = inp[rows, :].astype(F32) / root[rows, 0:1]
        nm[0, rows, :] = (unit * gain_own).astype(BF16)

    nm_made = gather_start(nm.at[0], nm_slots)

    up_made["rb"].wait_recv()
    take_upstream(1)
    out_terms(1)
    up_made["la"].wait_recv()
    take_upstream(2)
    out_terms(2)
    up_made["fa"].wait_recv()
    up_made["fb"].wait_recv()
    take_upstream(3)

    @pl.loop(0, 16)
    def _(i):
        rows = rows_of(i, 32)
        ag[rows, :] = aga[rows, :].astype(BF16)

    @pl.loop(0, 4)
    def _(i):
        m = lax.div(i, 2)
        group = lax.rem(i, 2)
        rows = rows_of(m, 256)
        lanes = rows_of(group, 128)
        key_grad = jnp.zeros((256, 128), F32)
        value_grad = jnp.zeros((256, 128), F32)
        for h in range(2):
            head = rows_of(group * 2 + h, 128)
            grad = ag[rows, head]
            weights = probs[i * 2 + h]
            probs_grad = dot(grad, v[rows, lanes], NT)
            row_dot = jnp.sum(weights * probs_grad, axis=-1, keepdims=True)
            score_grad = (weights * (probs_grad - row_dot) * SCALE).astype(BF16)
            at = rows_of(group * 4 + h, 128)
            qk[rows, at] = dot(score_grad, k[rows, lanes], NN).astype(BF16)
            key_grad += dot(score_grad, q[rows, head], TN)
            value_grad += dot(weights.astype(BF16), grad, TN)
        qk[rows, rows_of(group * 4 + 2, 128)] = key_grad.astype(BF16)
        qk[rows, rows_of(group * 4 + 3, 128)] = value_grad.astype(BF16)

    loads[4].wait()

    q_made = {}

    def qkv_terms(slot):
        block = lax.rem(z + offsets[slot], 4)

        @pl.loop(0, 4)
        def _(j):
            target = lax.rem(x + j, 4)
            lanes = rows_of(target, 256)
            term = dot(nm[slot, :, lanes], qk[...], TN)
            weighted = jnp.sum(term * wq[block, lanes, :].astype(F32), axis=-1, keepdims=True)
            gp[slot, :, lanes] = as_row(weighted)
            q_s[slot, j] = term.astype(BF16)

        q_made[slot] = scatter(
            q_s.at[slot, 2], q_s.at[slot, 1], q_s.at[slot, 3], 128, q_x1.at[slot], q_x2.at[slot], x_to
        )
        scatter_start(q_made[slot])

    def qkv_mid(slot):
        scatter_mid(q_made[slot])

    def qkv_end(slot):
        block = lax.rem(z + offsets[slot], 4)
        scatter_wait(q_made[slot])

        @pl.loop(0, 8)
        def _(i):
            rows = rows_of(i, 32)
            total = (
                q_s[slot, 0, rows, :].astype(F32)
                + q_x2[slot, 0, rows, :].astype(F32)
                + q_x2[slot, 1, rows, :].astype(F32)
            )
            q_y[block, rows, :] = total.astype(BF16)

    qkv_terms(0)
    out_terms(3)
    o_made = scatter(
        o_s.at[lax.rem(y + 2, 4)], o_s.at[lax.rem(y + 1, 4)], o_s.at[lax.rem(y + 3, 4)],
        256, o_y1, o_y2, y_to,
    )
    scatter_start(o_made)
    gather_relay(nm_made, nm_slots)
    qkv_mid(0)

    z_made = scatter(wo.at[2], wo.at[1], wo.at[3], 256, g_1, g_2, z_to, keep=False)

    @pl.when(sec == 1)
    def _():
        @pl.loop(0, 16)
        def _(i):
            j = lax.div(i, 4)
            part = rows_of(lax.rem(i, 4), 256)
            term = dot(qk[...], wq[lax.rem(z + j, 4), part, :], NT)
            wo[j, :, part] = term.astype(BF16)

        scatter_start(z_made)

    nm_made["rb"].wait_recv()
    qkv_terms(1)
    nm_made["la"].wait_recv()
    qkv_terms(2)
    scatter_mid(o_made)
    qkv_mid(1)
    qkv_mid(2)
    nm_made["fa"].wait_recv()
    nm_made["fb"].wait_recv()
    qkv_terms(3)

    gz_made = [
        copy(gp.at[slot], gz.at[slot - 1], z_to[offsets[slot]]) for slot in (1, 2, 3)
    ]
    for one in gz_made:
        one.start()
    qkv_end(0)

    scatter_wait(o_made)
    o_own = o_s.at[y]

    @pl.loop(0, 4)
    def _(j):
        lanes = rows_of(lax.rem(x + j, 4), 256)

        @pl.loop(0, 8)
        def _(i):
            rows = rows_of(i, 64)
            total = (
                o_own[rows, lanes].astype(F32)
                + o_y2[0, rows, lanes].astype(F32)
                + o_y2[1, rows, lanes].astype(F32)
            )
            o_x[j, rows, :] = total.astype(BF16)

    ox_made = scatter(o_x.at[2], o_x.at[1], o_x.at[3], 256, o_x1, o_x2, x_to)
    scatter_start(ox_made)

    for one in gz_made:
        one.wait_recv()
    gx[0] = gp[0] + gz[0] + gz[1] + gz[2]
    gx_made = [copy(gx.at[0], gx.at[s], x_to[s]) for s in (1, 2, 3)]
    for one in gx_made:
        one.start()

    qkv_mid(3)

    @pl.when(sec == 1)
    def _():
        scatter_mid(z_made)

    scatter_mid(ox_made)
    qkv_end(1)
    qkv_end(2)

    for one in gx_made:
        one.wait_recv()
    gy[0] = gx[0] + gx[1] + gx[2] + gx[3]
    gy_made = [copy(gy.at[0], gy.at[s], y_to[s]) for s in (1, 2, 3)]
    for one in gy_made:
        one.start()

    qkv_end(3)
    qy_made = scatter(
        q_y.at[lax.rem(y + 2, 4)], q_y.at[lax.rem(y + 1, 4)], q_y.at[lax.rem(y + 3, 4)],
        128, q_y1, q_y2, y_to,
    )
    scatter_start(qy_made)

    layer = upb.at[2]
    row_made = [copy(rowp.at[0], rowp.at[s], z_to[s], keep=False) for s in (1, 2, 3)]

    def scaled_unit(rows):
        grad = (
            wo[0, rows, :].astype(F32) + g_2[0, rows, :].astype(F32) + g_2[1, rows, :].astype(F32)
        )
        return grad * gain_own, inp[rows, :].astype(F32) / root[rows, 0:1]

    @pl.when(sec == 1)
    def _():
        scatter_wait(z_made)

        @pl.loop(0, 16)
        def _(i):
            rows = rows_of(i, 32)
            scaled, unit = scaled_unit(rows)
            part = jnp.sum(scaled * unit, axis=-1, keepdims=True)
            rtot[rows, :] = jnp.broadcast_to(part, (32, 128))

        for m in range(2):
            lanes = pl.ds(256 * m, 256)
            rowp[0, :, lanes] = rtot[lanes, :].T[0:8, :]
        for one in row_made:
            one.start()

    scatter_mid(qy_made)

    passed_made = copy(layer, passed, other, keep=False)

    @pl.when(sec == 1)
    def _():
        for one in row_made:
            one.wait_recv()
        for m in range(2):
            lanes = pl.ds(256 * m, 256)
            total = rowp[0, :, lanes] + rowp[1, :, lanes] + rowp[2, :, lanes] + rowp[3, :, lanes]
            rtot[lanes, :] = as_column((total * (1.0 / 4096))[0:1, :])
        straight = order[0:1, 0:1] == 0.0

        @pl.loop(0, 16)
        def _(i):
            both = []
            for m in range(2):
                rows = pl.ds(pl.multiple_of(m * 256 + i * 16, 16), 16)
                scaled, unit = scaled_unit(rows)
                through = up[rows, :].astype(F32) + (scaled - unit * rtot[rows, 0:1]) / root[rows, 0:1]
                both.append(through)
            low, high = both
            keep_order = jnp.broadcast_to(straight, (16, 1024))
            rows = pl.ds(pl.multiple_of(i * 16, 16), 16)
            layer[rows, :] = jnp.where(keep_order, low, high).astype(BF16)
            rows = pl.ds(pl.multiple_of(256 + i * 16, 16), 16)
            layer[rows, :] = jnp.where(keep_order, high, low).astype(BF16)

        passed_made.start()

        @pl.loop(0, 16)
        def _(i):
            passed[rows_of(i, 32), :] = jnp.zeros((32, 1024), BF16)

    scatter_wait(ox_made)

    @pl.loop(0, 8)
    def _(i):
        rows = rows_of(i, 64)
        total = o_x[0, rows, :].astype(F32) + o_x2[0, rows, :].astype(F32) + o_x2[1, rows, :].astype(F32)
        og[rows, :] = total * (1.0 / 16)

    for one in gy_made:
        one.wait_recv()
    gg[...] = (gy[0] + gy[1] + gy[2] + gy[3]) / (gain_own * 16.0)

    scatter_wait(qy_made)

    @pl.loop(0, 8)
    def _(i):
        rows = rows_of(i, 32)
        total = q_y[y, rows, :].astype(F32) + q_y2[0, rows, :].astype(F32) + q_y2[1, rows, :].astype(F32)
        qg[rows, :] = total * (1.0 / 16)

    @pl.when(sec == 0)
    def _():
        passed_made.wait_recv()

    @pl.when(sec == 1)
    def _():
        for one in [z_made[name] for name in "abrl"] + row_made + [passed_made]:
            one.wait_send()

    for one in sent:
        one.wait_send()


def shards(
    layer_input,
    norm_gain,
    upstream_grad,
    saved_queries,
    saved_keys,
    saved_values,
    segment_ids,
    batch_order,
    qkv_weight,
    out_weight,
):
    def by_micro(array):
        return array[0].transpose(1, 0, 2).reshape(512, array.shape[3])

    order = jnp.broadcast_to(batch_order[0].astype(F32)[:, 0:1], (8, 128))
    vmem = pl.BlockSpec(memory_space=pltpu.VMEM)
    hbm = pl.BlockSpec(memory_space=pl.ANY)
    passed, qkv_grad, out_grad, gain_grad = pl.pallas_call(
        kernel,
        out_shape=(
            jax.ShapeDtypeStruct((512, 1024), BF16),
            jax.ShapeDtypeStruct((256, 1024), F32),
            jax.ShapeDtypeStruct((512, 256), F32),
            jax.ShapeDtypeStruct((8, 1024), F32),
        ),
        in_specs=[vmem] * 8 + [hbm] * 2,
        out_specs=(vmem,) * 4,
        scratch_shapes=[
            pltpu.VMEM((3, 512, 1024), BF16),
            pltpu.VMEM((4, 512, 1024), BF16),
            pltpu.VMEM((4, 512, 1024), BF16),
            pltpu.VMEM((4, 1024, 1024), BF16),
            pltpu.VMEM((8, 256, 256), F32),
            pltpu.VMEM((512, 512), BF16),
            pltpu.VMEM((512, 512), F32),
            pltpu.VMEM((512, 512), BF16),
            pltpu.VMEM((512, 1024), BF16),
            pltpu.VMEM((4, 512, 1024), BF16),
            pltpu.VMEM((2, 256, 1024), BF16),
            pltpu.VMEM((2, 512, 1024), BF16),
            pltpu.VMEM((4, 512, 256), BF16),
            pltpu.VMEM((2, 256, 256), BF16),
            pltpu.VMEM((2, 512, 256), BF16),
            pltpu.VMEM((4, 4, 256, 1024), BF16),
            pltpu.VMEM((4, 2, 128, 1024), BF16),
            pltpu.VMEM((4, 2, 256, 1024), BF16),
            pltpu.VMEM((4, 256, 1024), BF16),
            pltpu.VMEM((2, 128, 1024), BF16),
            pltpu.VMEM((2, 256, 1024), BF16),
            pltpu.VMEM((2, 256, 1024), BF16),
            pltpu.VMEM((2, 512, 1024), BF16),
            pltpu.VMEM((4, 8, 512), F32),
            pltpu.VMEM((4, 8, 512), F32),
            pltpu.VMEM((512, 128), F32),
            pltpu.VMEM((512, 128), F32),
            pltpu.VMEM((512, 256), F32),
            pltpu.VMEM((4, 8, 1024), F32),
            pltpu.VMEM((3, 8, 1024), F32),
            pltpu.VMEM((4, 8, 1024), F32),
            pltpu.VMEM((4, 8, 1024), F32),
            pltpu.SemaphoreType.DMA((5,)),
            pltpu.SemaphoreType.DMA((80,)),
            pltpu.SemaphoreType.DMA((80,)),
        ],
        compiler_params=pltpu.CompilerParams(
            collective_id=0, has_side_effects=True, vmem_limit_bytes=67043328
        ),
    )(
        by_micro(upstream_grad),
        by_micro(layer_input),
        by_micro(saved_queries),
        by_micro(saved_keys),
        by_micro(saved_values),
        segment_ids[0],
        norm_gain,
        order,
        qkv_weight[0].reshape(4, 1024, 1024),
        out_weight[0],
    )
    passed = passed.reshape(2, 256, 1024).transpose(1, 0, 2)
    return (passed[None], qkv_grad[None], out_grad[None], gain_grad[0:1])


def solution(mesh):
    placed = (
        P("section", "dp", None, "tensor"),
        P("section", None),
        P("section", "dp", None, "tensor"),
        P("section", "dp", None, "tensor"),
        P("section", "dp", None, "tensor"),
        P("section", "dp", None, "tensor"),
        P("section", None, "dp"),
        P("section", "dp", None),
        P("section", None, "tensor"),
        P("section", "tensor", None),
    )
    return jax.shard_map(
        shards,
        mesh=mesh,
        in_specs=placed,
        out_specs=(
            P("section", "dp", None, "tensor"),
            P("section", "dp", "tensor"),
            P("section", "tensor", "dp"),
            P("section", "tensor"),
        ),
        check_vma=False,
    )
```

time: 407 us -> 171 us (0.42)
  waiting for transfers between devices: 266 us -> 0 us
  Pallas kernels: 0 us -> 149 us
  blocking collectives: 49.5 us -> 0 us
  matrix products: 44.8 us -> 0 us
  other arithmetic: 20.8 us -> 0.66 us
  between operations: 14 us -> 0.64 us
  local copies, waits for them, and re-layouts: 9.73 us -> 19.6 us
    reduce_scatter x3 -> x0, waiting for transfers between devices: 204 us -> none  [the longest x1 109 us: shards(): lax.psum_scatter(qkv_total, 'dp', scatter_dimension=0, tiled=True)]
    pallas_call x0 -> x1, Pallas kernels: none -> 149 us  [shards(): pl.pallas_call(kernel, out_shape=(jax.ShapeDtypeStruct((512, 1024), BF16)...]
    all_gather x2 -> x0, waiting for transfers between devices: 61.5 us -> none  [the longest x1 45.9 us: layer_back(): lax.all_gather(upstream, 'tensor', axis=2, tiled=True)]
    psum x2 -> x0, blocking collectives: 49.5 us -> none  [the longest x1 40.9 us: shards(): gain_grad = lax.psum(gain_part, 'dp') / replicas]
    dot_general x9 -> x0, matrix products: 42.4 us -> none  [the longest x1 10.3 us: layer_back(): jnp.einsum('ibc,dc->ibd', qkv_grads, weights_qkv, preferred_element_type=...]
    transpose x0 -> x5, local copies, waits for them, and re-layouts: none -> 10.2 us  [by_micro(): return array[0].transpose(1, 0, 2).reshape(512, array.shape[3])]
    div x2 -> x0, other arithmetic: 7.3 us -> none  [the longest x1 6.7 us: layer_back(): unit_rows = widened / root_mean]
    reduce_sum x2 -> x0, other arithmetic: 6.12 us -> none  [the longest x1 3.23 us: layer_back(): jnp.mean(widened * widened, axis=-1, keepdims=True) + EPS]
  transfers between devices with their start and end apart: 6 -> 0, of which waited for: 5 -> 0; matrix products, arithmetic and copies ran while one was open for 17% -> 0% of each run, Pallas kernels for 0% -> 0%
where the time goes in v1:
time: 171 us; the launch traced here: 170 us
  Pallas kernels  149 us (87%)
  local copies, waits for them, and re-layouts  19.6 us (11%)
    pallas_call x1, Pallas kernels, shards(): pl.pallas_call(kernel, out_shape=(jax.ShapeDtypeStruct((512, 1024), BF16)...  149 us
    transpose x5, local copies, waits for them, and re-layouts, by_micro(): return array[0].transpose(1, 0, 2).reshape(512, array.shape[3])  10.2 us
    unnamed x2, local copies, waits for them, and re-layouts  4.17 us

profile of v1, /device:TPU:0, one launch (start us, length us, event | category | flops | bytes accessed | tf_op | source)
XLA Modules:
  0.0 170.0 jit_solution(3080728832889997106)
XLA Ops:
  0.6 0.7 convert_bitcast_fusion
  1.3 0.6 broadcast_in_dim.17.order
  1.9 1.7 copy.17
  3.6 1.7 %copy.18 = bf16[2,256,256]{2,1,0:T(8,128)(2,1)} copy(bf16[2,256,256]{2,0,1:T(2,128)(2,1)} %bitcast.50) | data formatting | bytes 524288 | tf_op jit(solution)/shard_map/transpose | solution.py:500
  5.3 1.9 %copy.16 = bf16[2,256,512]{2,1,0:T(8,128)(2,1)} copy(bf16[2,256,512]{2,0,1:T(2,128)(2,1)} %bitcast.47) | data formatting | bytes 1048576 | tf_op jit(solution)/shard_map/transpose | solution.py:500
  7.2 2.5 %copy.15 = bf16[2,256,1024]{2,1,0:T(8,128)(2,1)} copy(bf16[2,256,1024]{2,0,1:T(2,128)(2,1)} %bitcast.42) | data formatting | bytes 2097152 | tf_op jit(solution)/shard_map/transpose | solution.py:500
  9.7 2.5 %copy.14 = bf16[2,256,1024]{2,1,0:T(8,128)(2,1)} copy(bf16[2,256,1024]{2,0,1:T(2,128)(2,1)} %bitcast.43) | data formatting | bytes 2097152 | tf_op jit(solution)/shard_map/transpose | solution.py:500
  12.1 149.0 %shard_map.129 = (bf16[512,1024]{1,0:T(8,128)(2,1)}, f32[256,1024]{1,0:T(8,128)}, f32[512,256]{1,0:T(8,128)}, f32[8,1024]{1,0:T(8,128)}) custom-call(bf16[512,1024]{1,0:T(8,128)(2,1)} %bitcast.38, bf16[512,1024]{1,0:T(8,128)(2,1)} %bitcast.37, bf16[512,512]{1,0:T(8,128)(2,1)} %bitcast.39, bf16[512,256]{1,0:T(8,128)(2,1)} %bitcast.40, ...), custom_call_target="tpu_custom_call" | custom-call | tf_op jit(solution)/shard_map/pallas_call | solution.py:505
  161.2 3.3 %copy.21 = bf16[2,256,1024]{2,0,1:T(2,128)(2,1)} copy(bf16[2,256,1024]{2,1,0:T(8,128)(2,1)} %bitcast.46) | data formatting | bytes 2097152 | tf_op jit(solution)/shard_map/reshape | solution.py:567
  164.5 1.4 slice.7
  165.8 2.3 %copy.24 = f32[1,256,1024]{2,1,0:T(8,128)} copy(f32[1,256,1024]{2,1,0:T(8,128)} %bitcast.45) | data formatting | bytes 2097152
  168.1 1.9 %copy.25 = f32[1,512,256]{2,1,0:T(8,128)} copy(f32[1,512,256]{2,1,0:T(8,128)} %bitcast.48) | data formatting | bytes 1048576

commit v2 on v1

--- a/solution.py
+++ b/solution.py
@@ -38,10 +38,10 @@
 def kernel(
     up, inp, q, k, v, seg, gain, order, wq_hbm, wo_hbm,
     passed, qg, og, gg,
-    upb, nm, wo, wq, probs, ao, aga, ag, qk,
+    upb, nms, nmz, wo, wq, probs, ao, aga, ag, qk,
     o_s, o_y1, o_y2, o_x, o_x1, o_x2,
-    q_s, q_x1, q_x2, q_y, q_y1, q_y2,
-    g_1, g_2, ssq, rowp, root, rtot, segc, gp, gz, gx, gy,
+    q_y, q_y1, q_y2,
+    g_1, g_2, ssq, rowp, root, rtot, segc, gp, gz, gy, gx,
     lsem, ssem, rsem,
 ):
     sec = lax.axis_index("section")
@@ -89,24 +89,30 @@
 
     first, second = pl.ds(0, 256), pl.ds(256, 256)
 
-    def gather_start(own, slots):
-        made = {
-            "ra": copy(own.at[first], slots[1].at[first], z_to[1]),
-            "lb": copy(own.at[second], slots[2].at[second], z_to[3]),
-            "rb": copy(own.at[second], slots[1].at[second], z_to[1]),
-            "la": copy(own.at[first], slots[2].at[first], z_to[3]),
+    def gather(slots, to, a, b):
+        own, right, far, left = slots
+        return {
+            "ra": copy(own.at[a], left.at[a], to[1]),
+            "lb": copy(own.at[b], right.at[b], to[3]),
+            "rb": copy(own.at[b], left.at[b], to[1]),
+            "la": copy(own.at[a], right.at[a], to[3]),
+            "fa": copy(left.at[a], far.at[a], to[1]),
+            "fb": copy(right.at[b], far.at[b], to[3]),
         }
+
+    def gather_start(made):
         for name in ("ra", "lb", "rb", "la"):
             made[name].start()
-        return made
-
-    def gather_relay(made, slots):
+
+    def gather_relay(made):
         made["ra"].wait_recv()
-        made["fa"] = copy(slots[1].at[first], slots[3].at[first], z_to[1])
         made["fa"].start()
         made["lb"].wait_recv()
-        made["fb"] = copy(slots[2].at[second], slots[3].at[second], z_to[3])
         made["fb"].start()
+
+    def gather_wait(made):
+        for name in ("rb", "la", "fa", "fb"):
+            made[name].wait_recv()
 
     def add_rows(dst, src, count, step=32):
         @pl.loop(0, count // step)
@@ -141,10 +147,8 @@
         made["l"].wait_recv()
 
     up_slots = [up, upb.at[0], upb.at[1], upb.at[2]]
-    nm_slots = [nm.at[0], nm.at[1], nm.at[2], nm.at[3]]
-    offsets = (0, 3, 1, 2)
-
-    up_made = gather_start(up, up_slots)
+    up_made = gather(up_slots, z_to, first, second)
+    gather_start(up_made)
 
     for m in range(2):
         total = jnp.zeros((256, 1), F32)
@@ -182,7 +186,7 @@
         one.wait()
 
     def take_upstream(slot):
-        block = lax.rem(z + offsets[slot], 4)
+        block = lax.rem(z + slot, 4)
         ref = up_slots[slot]
 
         @pl.loop(0, 2)
@@ -195,7 +199,7 @@
                 aga[rows, :] += term
 
     def out_terms(slot):
-        block = lax.rem(z + offsets[slot], 4)
+        block = lax.rem(z + slot, 4)
         ref = up_slots[slot]
 
         @pl.loop(0, 4)
@@ -204,109 +208,113 @@
             o_s[block, :, lanes] = dot(ao[...], ref[:, lanes], TN).astype(BF16)
 
     take_upstream(0)
+    gather_relay(up_made)
     out_terms(0)
-    gather_relay(up_made, up_slots)
 
     for one in ssq_made:
         one.wait_recv()
-    gain_own = gain[:, pl.ds(pl.multiple_of(z * 1024, 1024), 1024)]
     for m in range(2):
         lanes = pl.ds(256 * m, 256)
         total = ssq[0, :, lanes] + ssq[1, :, lanes] + ssq[2, :, lanes] + ssq[3, :, lanes]
         root[lanes, :] = as_column(jnp.sqrt(total * (1.0 / 4096) + EPS)[0:1, :])
 
-    @pl.loop(0, 16)
-    def _(i):
-        rows = rows_of(i, 32)
-        unit = inp[rows, :].astype(F32) / root[rows, 0:1]
-        nm[0, rows, :] = (unit * gain_own).astype(BF16)
-
-    nm_made = gather_start(nm.at[0], nm_slots)
+    for j in range(4):
+        target = lax.rem(x + j, 4)
+        lanes = rows_of(target, 256)
+        part = gain[:, rows_of(z * 4 + target, 256)]
+        kept = nmz.at[0, 0] if j == 0 else nms.at[j - 1]
+
+        @pl.loop(0, 8)
+        def _(i):
+            rows = rows_of(i, 64)
+            unit = inp[rows, lanes].astype(F32) / root[rows, 0:1]
+            kept[rows, :] = (unit * part).astype(BF16)
+
+    nx_made = [copy(nms.at[j - 1], nmz.at[0, 4 - j], x_to[j]) for j in (1, 2, 3)]
+    for one in nx_made:
+        one.start()
 
     up_made["rb"].wait_recv()
+    take_upstream(3)
+    out_terms(3)
+    up_made["la"].wait_recv()
     take_upstream(1)
     out_terms(1)
-    up_made["la"].wait_recv()
-    take_upstream(2)
-    out_terms(2)
+
+    for one in nx_made:
+        one.wait_recv()
+    nm_made = gather([nmz.at[r] for r in range(4)], z_to, pl.ds(0, 2), pl.ds(2, 2))
+    gather_start(nm_made)
+
     up_made["fa"].wait_recv()
     up_made["fb"].wait_recv()
-    take_upstream(3)
+    take_upstream(2)
 
     @pl.loop(0, 16)
     def _(i):
         rows = rows_of(i, 32)
         ag[rows, :] = aga[rows, :].astype(BF16)
 
-    @pl.loop(0, 4)
-    def _(i):
-        m = lax.div(i, 2)
-        group = lax.rem(i, 2)
-        rows = rows_of(m, 256)
-        lanes = rows_of(group, 128)
-        key_grad = jnp.zeros((256, 128), F32)
-        value_grad = jnp.zeros((256, 128), F32)
-        for h in range(2):
-            head = rows_of(group * 2 + h, 128)
-            grad = ag[rows, head]
-            weights = probs[i * 2 + h]
-            probs_grad = dot(grad, v[rows, lanes], NT)
-            row_dot = jnp.sum(weights * probs_grad, axis=-1, keepdims=True)
-            score_grad = (weights * (probs_grad - row_dot) * SCALE).astype(BF16)
-            at = rows_of(group * 4 + h, 128)
-            qk[rows, at] = dot(score_grad, k[rows, lanes], NN).astype(BF16)
-            key_grad += dot(score_grad, q[rows, head], TN)
-            value_grad += dot(weights.astype(BF16), grad, TN)
-        qk[rows, rows_of(group * 4 + 2, 128)] = key_grad.astype(BF16)
-        qk[rows, rows_of(group * 4 + 3, 128)] = value_grad.astype(BF16)
-
-    loads[4].wait()
-
-    q_made = {}
-
-    def qkv_terms(slot):
-        block = lax.rem(z + offsets[slot], 4)
-
-        @pl.loop(0, 4)
-        def _(j):
-            target = lax.rem(x + j, 4)
-            lanes = rows_of(target, 256)
-            term = dot(nm[slot, :, lanes], qk[...], TN)
-            weighted = jnp.sum(term * wq[block, lanes, :].astype(F32), axis=-1, keepdims=True)
-            gp[slot, :, lanes] = as_row(weighted)
-            q_s[slot, j] = term.astype(BF16)
-
-        q_made[slot] = scatter(
-            q_s.at[slot, 2], q_s.at[slot, 1], q_s.at[slot, 3], 128, q_x1.at[slot], q_x2.at[slot], x_to
-        )
-        scatter_start(q_made[slot])
-
-    def qkv_mid(slot):
-        scatter_mid(q_made[slot])
-
-    def qkv_end(slot):
-        block = lax.rem(z + offsets[slot], 4)
-        scatter_wait(q_made[slot])
-
-        @pl.loop(0, 8)
-        def _(i):
-            rows = rows_of(i, 32)
-            total = (
-                q_s[slot, 0, rows, :].astype(F32)
-                + q_x2[slot, 0, rows, :].astype(F32)
-                + q_x2[slot, 1, rows, :].astype(F32)
-            )
-            q_y[block, rows, :] = total.astype(BF16)
-
-    qkv_terms(0)
-    out_terms(3)
+    qk_made = [
+        gather([qk.at[group, r] for r in range(4)], x_to, first, second) for group in range(2)
+    ]
+    for group in range(2):
+        lanes = pl.ds(128 * group, 128)
+
+        @pl.loop(0, 2)
+        def _(m):
+            rows = rows_of(m, 256)
+            key_grad = jnp.zeros((256, 128), F32)
+            value_grad = jnp.zeros((256, 128), F32)
+            for h in range(2):
+                head = pl.ds(128 * (group * 2 + h), 128)
+                grad = ag[rows, head]
+                weights = probs[m * 4 + group * 2 + h]
+                probs_grad = dot(grad, v[rows, lanes], NT)
+                row_dot = jnp.sum(weights * probs_grad, axis=-1, keepdims=True)
+                score_grad = (weights * (probs_grad - row_dot) * SCALE).astype(BF16)
+                qk[group, 0, rows, pl.ds(128 * h, 128)] = dot(score_grad, k[rows, lanes], NN).astype(BF16)
+                key_grad += dot(score_grad, q[rows, head], TN)
+                value_grad += dot(weights.astype(BF16), grad, TN)
+            qk[group, 0, rows, pl.ds(256, 128)] = key_grad.astype(BF16)
+            qk[group, 0, rows, pl.ds(384, 128)] = value_grad.astype(BF16)
+
+        gather_start(qk_made[group])
+
+    gather_relay(nm_made)
+    out_terms(2)
     o_made = scatter(
         o_s.at[lax.rem(y + 2, 4)], o_s.at[lax.rem(y + 1, 4)], o_s.at[lax.rem(y + 3, 4)],
         256, o_y1, o_y2, y_to,
     )
     scatter_start(o_made)
-    gather_relay(nm_made, nm_slots)
-    qkv_mid(0)
+    gather_relay(qk_made[0])
+    loads[4].wait()
+
+    q_made = [
+        scatter(
+            q_y.at[group, lax.rem(y + 2, 4)], q_y.at[group, lax.rem(y + 1, 4)],
+            q_y.at[group, lax.rem(y + 3, 4)], 128, q_y1.at[group], q_y2.at[group], y_to,
+        )
+        for group in range(2)
+    ]
+
+    def qkv_terms(group):
+        def one(j):
+            block = lax.rem(y + j + 2, 4)
+            slot = lax.rem(block - z + 4, 4)
+            term = dot(nmz[slot].reshape(2048, 256), qk[group].reshape(2048, 512), TN)
+            weight = wq[block, rows_of(x, 256), pl.ds(512 * group, 512)].astype(F32)
+            row = as_row(jnp.sum(term * weight, axis=-1, keepdims=True))
+            if group == 0:
+                gp[slot] = row
+            else:
+                gp[slot] += row
+            q_y[group, block] = term.astype(BF16)
+
+        one(0)
+        scatter_start(q_made[group])
+        pl.loop(1, 4)(one)
 
     z_made = scatter(wo.at[2], wo.at[1], wo.at[3], 256, g_1, g_2, z_to, keep=False)
 
@@ -316,28 +324,29 @@
         def _(i):
             j = lax.div(i, 4)
             part = rows_of(lax.rem(i, 4), 256)
-            term = dot(qk[...], wq[lax.rem(z + j, 4), part, :], NT)
+            at = lax.rem(z + j, 4)
+            term = dot(qk[0, 0], wq[at, part, pl.ds(0, 512)], NT)
+            term += dot(qk[1, 0], wq[at, part, pl.ds(512, 512)], NT)
             wo[j, :, part] = term.astype(BF16)
 
         scatter_start(z_made)
 
-    nm_made["rb"].wait_recv()
+    gather_relay(qk_made[1])
+    scatter_mid(o_made)
+    gather_wait(nm_made)
+    gather_wait(qk_made[0])
+    qkv_terms(0)
+
+    @pl.when(sec == 1)
+    def _():
+        scatter_mid(z_made)
+
+    gather_wait(qk_made[1])
     qkv_terms(1)
-    nm_made["la"].wait_recv()
-    qkv_terms(2)
-    scatter_mid(o_made)
-    qkv_mid(1)
-    qkv_mid(2)
-    nm_made["fa"].wait_recv()
-    nm_made["fb"].wait_recv()
-    qkv_terms(3)
-
-    gz_made = [
-        copy(gp.at[slot], gz.at[slot - 1], z_to[offsets[slot]]) for slot in (1, 2, 3)
-    ]
+
+    gz_made = [copy(gp.at[r], gz.at[r - 1], z_to[r]) for r in (1, 2, 3)]
     for one in gz_made:
         one.start()
-    qkv_end(0)
 
     scatter_wait(o_made)
     o_own = o_s.at[y]
@@ -358,46 +367,23 @@
 
     ox_made = scatter(o_x.at[2], o_x.at[1], o_x.at[3], 256, o_x1, o_x2, x_to)
     scatter_start(ox_made)
+    scatter_mid(q_made[0])
 
     for one in gz_made:
         one.wait_recv()
-    gx[0] = gp[0] + gz[0] + gz[1] + gz[2]
-    gx_made = [copy(gx.at[0], gx.at[s], x_to[s]) for s in (1, 2, 3)]
-    for one in gx_made:
-        one.start()
-
-    qkv_mid(3)
-
-    @pl.when(sec == 1)
-    def _():
-        scatter_mid(z_made)
-
-    scatter_mid(ox_made)
-    qkv_end(1)
-    qkv_end(2)
-
-    for one in gx_made:
-        one.wait_recv()
-    gy[0] = gx[0] + gx[1] + gx[2] + gx[3]
+    gy[0] = gp[0] + gz[0] + gz[1] + gz[2]
     gy_made = [copy(gy.at[0], gy.at[s], y_to[s]) for s in (1, 2, 3)]
     for one in gy_made:
         one.start()
 
-    qkv_end(3)
-    qy_made = scatter(
-        q_y.at[lax.rem(y + 2, 4)], q_y.at[lax.rem(y + 1, 4)], q_y.at[lax.rem(y + 3, 4)],
-        128, q_y1, q_y2, y_to,
-    )
-    scatter_start(qy_made)
-
-    layer = upb.at[2]
+    layer = upb.at[1]
     row_made = [copy(rowp.at[0], rowp.at[s], z_to[s], keep=False) for s in (1, 2, 3)]
 
     def scaled_unit(rows):
         grad = (
             wo[0, rows, :].astype(F32) + g_2[0, rows, :].astype(F32) + g_2[1, rows, :].astype(F32)
         )
-        return grad * gain_own, inp[rows, :].astype(F32) / root[rows, 0:1]
+        return grad * gain[:, rows_of(z, 1024)], inp[rows, :].astype(F32) / root[rows, 0:1]
 
     @pl.when(sec == 1)
     def _():
@@ -416,7 +402,15 @@
         for one in row_made:
             one.start()
 
-    scatter_mid(qy_made)
+    scatter_mid(ox_made)
+    scatter_mid(q_made[1])
+
+    for one in gy_made:
+        one.wait_recv()
+    gx[x] = (gy[0] + gy[1] + gy[2] + gy[3]) / (gain[:, rows_of(z * 4 + x, 256)] * 16.0)
+    gx_made = [copy(gx.at[x], gx.at[x], x_to[s]) for s in (1, 2, 3)]
+    for one in gx_made:
+        one.start()
 
     passed_made = copy(layer, passed, other, keep=False)
 
@@ -428,7 +422,7 @@
             lanes = pl.ds(256 * m, 256)
             total = rowp[0, :, lanes] + rowp[1, :, lanes] + rowp[2, :, lanes] + rowp[3, :, lanes]
             rtot[lanes, :] = as_column((total * (1.0 / 4096))[0:1, :])
-        straight = order[0:1, 0:1] == 0.0
+        straight = order[0:1, 0:1] == 0
 
         @pl.loop(0, 16)
         def _(i):
@@ -459,17 +453,23 @@
         total = o_x[0, rows, :].astype(F32) + o_x2[0, rows, :].astype(F32) + o_x2[1, rows, :].astype(F32)
         og[rows, :] = total * (1.0 / 16)
 
-    for one in gy_made:
+    for one in gx_made:
         one.wait_recv()
-    gg[...] = (gy[0] + gy[1] + gy[2] + gy[3]) / (gain_own * 16.0)
-
-    scatter_wait(qy_made)
-
-    @pl.loop(0, 8)
-    def _(i):
-        rows = rows_of(i, 32)
-        total = q_y[y, rows, :].astype(F32) + q_y2[0, rows, :].astype(F32) + q_y2[1, rows, :].astype(F32)
-        qg[rows, :] = total * (1.0 / 16)
+    for s in range(4):
+        gg[:, pl.ds(256 * s, 256)] = gx[s]
+
+    for group in range(2):
+        scatter_wait(q_made[group])
+
+        @pl.loop(0, 4)
+        def _(i):
+            rows = rows_of(i, 64)
+            total = (
+                q_y[group, y, rows, :].astype(F32)
+                + q_y2[group, 0, rows, :].astype(F32)
+                + q_y2[group, 1, rows, :].astype(F32)
+            )
+            qg[rows, pl.ds(512 * group, 512)] = total * (1.0 / 16)
 
     @pl.when(sec == 0)
     def _():
@@ -499,7 +499,6 @@
     def by_micro(array):
         return array[0].transpose(1, 0, 2).reshape(512, array.shape[3])
 
-    order = jnp.broadcast_to(batch_order[0].astype(F32)[:, 0:1], (8, 128))
     vmem = pl.BlockSpec(memory_space=pltpu.VMEM)
     hbm = pl.BlockSpec(memory_space=pl.ANY)
     passed, qkv_grad, out_grad, gain_grad = pl.pallas_call(
@@ -514,26 +513,24 @@
         out_specs=(vmem,) * 4,
         scratch_shapes=[
             pltpu.VMEM((3, 512, 1024), BF16),
-            pltpu.VMEM((4, 512, 1024), BF16),
+            pltpu.VMEM((3, 512, 256), BF16),
+            pltpu.VMEM((4, 4, 512, 256), BF16),
             pltpu.VMEM((4, 512, 1024), BF16),
             pltpu.VMEM((4, 1024, 1024), BF16),
             pltpu.VMEM((8, 256, 256), F32),
             pltpu.VMEM((512, 512), BF16),
             pltpu.VMEM((512, 512), F32),
             pltpu.VMEM((512, 512), BF16),
-            pltpu.VMEM((512, 1024), BF16),
+            pltpu.VMEM((2, 4, 512, 512), BF16),
             pltpu.VMEM((4, 512, 1024), BF16),
             pltpu.VMEM((2, 256, 1024), BF16),
             pltpu.VMEM((2, 512, 1024), BF16),
             pltpu.VMEM((4, 512, 256), BF16),
             pltpu.VMEM((2, 256, 256), BF16),
             pltpu.VMEM((2, 512, 256), BF16),
-            pltpu.VMEM((4, 4, 256, 1024), BF16),
-            pltpu.VMEM((4, 2, 128, 1024), BF16),
-            pltpu.VMEM((4, 2, 256, 1024), BF16),
-            pltpu.VMEM((4, 256, 1024), BF16),
-            pltpu.VMEM((2, 128, 1024), BF16),
-            pltpu.VMEM((2, 256, 1024), BF16),
+            pltpu.VMEM((2, 4, 256, 512), BF16),
+            pltpu.VMEM((2, 2, 128, 512), BF16),
+            pltpu.VMEM((2, 2, 256, 512), BF16),
             pltpu.VMEM((2, 256, 1024), BF16),
             pltpu.VMEM((2, 512, 1024), BF16),
             pltpu.VMEM((4, 8, 512), F32),
@@ -541,10 +538,10 @@
             pltpu.VMEM((512, 128), F32),
             pltpu.VMEM((512, 128), F32),
             pltpu.VMEM((512, 256), F32),
-            pltpu.VMEM((4, 8, 1024), F32),
-            pltpu.VMEM((3, 8, 1024), F32),
-            pltpu.VMEM((4, 8, 1024), F32),
-            pltpu.VMEM((4, 8, 1024), F32),
+            pltpu.VMEM((4, 8, 256), F32),
+            pltpu.VMEM((3, 8, 256), F32),
+            pltpu.VMEM((4, 8, 256), F32),
+            pltpu.VMEM((4, 8, 256), F32),
             pltpu.SemaphoreType.DMA((5,)),
             pltpu.SemaphoreType.DMA((80,)),
             pltpu.SemaphoreType.DMA((80,)),
@@ -560,7 +557,7 @@
         by_micro(saved_values),
         segment_ids[0],
         norm_gain,
-        order,
+        batch_order[0],
         qkv_weight[0].reshape(4, 1024, 1024),
         out_weight[0],
     )

time: 171 us -> 139 us (0.81)
  Pallas kernels: 149 us -> 118 us
    pallas_call x1, Pallas kernels: 149 us -> 118 us  [shards(): pl.pallas_call(kernel, out_shape=(jax.ShapeDtypeStruct((512, 1024), BF16)...]
where the time goes in v2:
time: 139 us; the launch traced here: 138 us
  Pallas kernels  118 us (85%)
  local copies, waits for them, and re-layouts  19 us (14%)
    pallas_call x1, Pallas kernels, shards(): pl.pallas_call(kernel, out_shape=(jax.ShapeDtypeStruct((512, 1024), BF16)...  118 us
    transpose x5, local copies, waits for them, and re-layouts, by_micro(): return array[0].transpose(1, 0, 2).reshape(512, array.shape[3])  10.2 us
    unnamed x2, local copies, waits for them, and re-layouts  4.17 us
    reshape x1, local copies, waits for them, and re-layouts, shards(): passed = passed.reshape(2, 256, 1024).transpose(1, 0, 2)  3.27 us

profile of v2, /device:TPU:0, one launch (start us, length us, event | category | flops | bytes accessed | tf_op | source)
XLA Modules:
  0.0 138.1 jit_solution(9285936274254265799)
XLA Ops:
  0.6 1.7 %copy.17 = bf16[2,256,256]{2,1,0:T(8,128)(2,1)} copy(bf16[2,256,256]{2,0,1:T(2,128)(2,1)} %bitcast.46) | data formatting | bytes 524288 | tf_op jit(solution)/shard_map/transpose | solution.py:500
  2.3 1.7 %copy.18 = bf16[2,256,256]{2,1,0:T(8,128)(2,1)} copy(bf16[2,256,256]{2,0,1:T(2,128)(2,1)} %bitcast.47) | data formatting | bytes 524288 | tf_op jit(solution)/shard_map/transpose | solution.py:500
  4.0 1.9 %copy.16 = bf16[2,256,512]{2,1,0:T(8,128)(2,1)} copy(bf16[2,256,512]{2,0,1:T(2,128)(2,1)} %bitcast.44) | data formatting | bytes 1048576 | tf_op jit(solution)/shard_map/transpose | solution.py:500
  5.9 2.5 %copy.15 = bf16[2,256,1024]{2,1,0:T(8,128)(2,1)} copy(bf16[2,256,1024]{2,0,1:T(2,128)(2,1)} %bitcast.39) | data formatting | bytes 2097152 | tf_op jit(solution)/shard_map/transpose | solution.py:500
  8.4 2.5 %copy.14 = bf16[2,256,1024]{2,1,0:T(8,128)(2,1)} copy(bf16[2,256,1024]{2,0,1:T(2,128)(2,1)} %bitcast.40) | data formatting | bytes 2097152 | tf_op jit(solution)/shard_map/transpose | solution.py:500
  10.8 118.4 %shard_map.129 = (bf16[512,1024]{1,0:T(8,128)(2,1)}, f32[256,1024]{1,0:T(8,128)}, f32[512,256]{1,0:T(8,128)}, f32[8,1024]{1,0:T(8,128)}) custom-call(bf16[512,1024]{1,0:T(8,128)(2,1)} %bitcast.34, bf16[512,1024]{1,0:T(8,128)(2,1)} %bitcast.33, bf16[512,512]{1,0:T(8,128)(2,1)} %bitcast.36, bf16[512,256]{1,0:T(8,128)(2,1)} %bitcast.37, ...), custom_call_target="tpu_custom_call" | custom-call | tf_op jit(solution)/shard_map/pallas_call | solution.py:504
  129.3 3.3 %copy.21 = bf16[2,256,1024]{2,0,1:T(2,128)(2,1)} copy(bf16[2,256,1024]{2,1,0:T(8,128)(2,1)} %bitcast.43) | data formatting | bytes 2097152 | tf_op jit(solution)/shard_map/reshape | solution.py:564
  132.6 1.4 slice.3
  133.9 2.3 %copy.24 = f32[1,256,1024]{2,1,0:T(8,128)} copy(f32[1,256,1024]{2,1,0:T(8,128)} %bitcast.42) | data formatting | bytes 2097152
  136.2 1.9 %copy.25 = f32[1,512,256]{2,1,0:T(8,128)} copy(f32[1,512,256]{2,1,0:T(8,128)} %bitcast.45) | data formatting | bytes 1048576

commit v3 on v2

--- a/solution.py
+++ b/solution.py
@@ -12,6 +12,7 @@
 MESH = pl.DeviceIdType.MESH
 F32 = jnp.float32
 BF16 = jnp.bfloat16
+SIX = ("fa", "fb", "rb", "la", "ra", "lb")
 SCALE = 1.0 / math.sqrt(HD)
 
 NT = (((1,), (1,)), ((), ()))
@@ -36,12 +37,13 @@
 
 
 def kernel(
-    up, inp, q, k, v, seg, gain, order, wq_hbm, wo_hbm,
+    up_hbm, inp_hbm, q_hbm, k_hbm, v_hbm, seg, gain, order, wq_hbm, wo_hbm,
     passed, qg, og, gg,
     upb, nms, nmz, wo, wq, probs, ao, aga, ag, qk,
     o_s, o_y1, o_y2, o_x, o_x1, o_x2,
     q_y, q_y1, q_y2,
     g_1, g_2, ssq, rowp, root, rtot, segc, gp, gz, gy, gx,
+    up_raw, inp_raw, q_raw, k_raw, v_raw, up, inp, q, k, v, un,
     lsem, ssem, rsem,
 ):
     sec = lax.axis_index("section")
@@ -73,13 +75,26 @@
             sent.append(made)
         return made
 
+    stored = ((up_hbm, up_raw, up), (inp_hbm, inp_raw, inp), (q_hbm, q_raw, q), (k_hbm, k_raw, k), (v_hbm, v_raw, v))
+    fetches = [
+        pltpu.make_async_copy(source, raw, lsem.at[5 + i]) for i, (source, raw, _) in enumerate(stored)
+    ]
     loads = [
         pltpu.make_async_copy(wo_hbm.at[:, pl.ds(1024 * b, 1024)], wo.at[b], lsem.at[b])
         for b in range(4)
     ]
     loads.append(pltpu.make_async_copy(wq_hbm, wq, lsem.at[4]))
-    for one in loads:
+    for one in fetches + loads:
         one.start()
+
+    def by_micro(which):
+        fetches[which].wait()
+        _, raw, kept = stored[which]
+
+        @pl.loop(0, 16)
+        def _(i):
+            for m in range(2):
+                kept[pl.ds(pl.multiple_of(256 * m + i * 16, 16), 16), :] = raw[rows_of(i, 16), m, :]
 
     barrier = pltpu.get_barrier_semaphore()
     peers = z_to[1:] + x_to[1:] + y_to[1:] + [other]
@@ -121,34 +136,46 @@
             dst[part, :] = (dst[part, :].astype(F32) + src[part, :].astype(F32)).astype(BF16)
 
     def scatter(far, right, left, half, land, full, to, keep=True):
+        a, b = pl.ds(0, half), pl.ds(half, half)
         return {
-            "a": copy(far.at[pl.ds(0, half)], land.at[0], to[1], keep),
-            "b": copy(far.at[pl.ds(half, half)], land.at[1], to[3], keep),
-            "r": copy(right, full.at[0], to[1], keep),
-            "l": copy(left, full.at[1], to[3], keep),
-            "add_a": (right.at[pl.ds(0, half)], land.at[0], half),
-            "add_b": (left.at[pl.ds(half, half)], land.at[1], half),
+            "fa": copy(far.at[a], land.at[0], to[1], keep),
+            "fb": copy(far.at[b], land.at[1], to[3], keep),
+            "rb": copy(right.at[b], full.at[0, b], to[1], keep),
+            "la": copy(left.at[a], full.at[1, a], to[3], keep),
+            "ra": copy(right.at[a], full.at[0, a], to[1], keep),
+            "lb": copy(left.at[b], full.at[1, b], to[3], keep),
+            "add_a": (right.at[a], land.at[0], half),
+            "add_b": (left.at[b], land.at[1], half),
         }
 
     def scatter_start(made):
-        made["a"].start()
-        made["b"].start()
+        for name in ("fa", "fb", "rb", "la"):
+            made[name].start()
+
+    def scatter_mid_a(made):
+        made["fa"].wait_recv()
+        add_rows(*made["add_a"])
+        made["ra"].start()
+
+    def scatter_mid_b(made):
+        made["fb"].wait_recv()
+        add_rows(*made["add_b"])
+        made["lb"].start()
 
     def scatter_mid(made):
-        made["a"].wait_recv()
-        add_rows(*made["add_a"])
-        made["r"].start()
-        made["b"].wait_recv()
-        add_rows(*made["add_b"])
-        made["l"].start()
+        scatter_mid_a(made)
+        scatter_mid_b(made)
 
     def scatter_wait(made):
-        made["r"].wait_recv()
-        made["l"].wait_recv()
+        for name in ("rb", "la", "ra", "lb"):
+            made[name].wait_recv()
 
     up_slots = [up, upb.at[0], upb.at[1], upb.at[2]]
     up_made = gather(up_slots, z_to, first, second)
-    gather_start(up_made)
+    by_micro(0)
+    up_made["ra"].start()
+    up_made["lb"].start()
+    by_micro(1)
 
     for m in range(2):
         total = jnp.zeros((256, 1), F32)
@@ -159,6 +186,10 @@
     ssq_made = [copy(ssq.at[0], ssq.at[s], z_to[s]) for s in (1, 2, 3)]
     for one in ssq_made:
         one.start()
+    up_made["rb"].start()
+    up_made["la"].start()
+    for which in (2, 3, 4):
+        by_micro(which)
 
     for m in range(2):
         ids = seg[pl.ds(m, 1), :].astype(F32)
@@ -180,7 +211,7 @@
         shifted = jnp.where(visible, jnp.exp(scores - top), 0.0)
         weights = shifted / jnp.sum(shifted, axis=-1, keepdims=True)
         probs[i] = weights
-        ao[rows, rows_of(head, 128)] = dot(weights.astype(BF16), v[rows, lanes], NN).astype(BF16)
+        ao[rows_of(head, 128), rows] = dot(weights.astype(BF16), v[rows, lanes], NN).T.astype(BF16)
 
     for one in loads[:4]:
         one.wait()
@@ -195,8 +226,15 @@
             term = dot(ref[rows, :], wo[block], NT)
             if slot == 0:
                 aga[rows, :] = term
+            elif slot == 2:
+                ag[rows, :] = (aga[rows, :] + term).astype(BF16)
             else:
                 aga[rows, :] += term
+
+    o_made = scatter(
+        o_s.at[lax.rem(y + 2, 4)], o_s.at[lax.rem(y + 1, 4)], o_s.at[lax.rem(y + 3, 4)],
+        256, o_y1, o_y2, y_to,
+    )
 
     def out_terms(slot):
         block = lax.rem(z + slot, 4)
@@ -205,18 +243,44 @@
         @pl.loop(0, 4)
         def _(j):
             lanes = rows_of(j, 256)
-            o_s[block, :, lanes] = dot(ao[...], ref[:, lanes], TN).astype(BF16)
+            o_s[block, :, lanes] = dot(ao[...], ref[:, lanes], NN).astype(BF16)
+
+        role = lax.rem(block - y + 4, 4)
+
+        @pl.when(role == 2)
+        def _():
+            o_made["fa"].start()
+            o_made["fb"].start()
+
+        @pl.when(role == 1)
+        def _():
+            o_made["rb"].start()
+
+        @pl.when(role == 3)
+        def _():
+            o_made["la"].start()
+
+    def out_mid(slot):
+        role = lax.rem(lax.rem(z + slot, 4) - y + 4, 4)
+
+        @pl.when(role == 1)
+        def _():
+            scatter_mid_a(o_made)
+
+        @pl.when(role == 3)
+        def _():
+            scatter_mid_b(o_made)
 
     take_upstream(0)
+    out_terms(0)
     gather_relay(up_made)
-    out_terms(0)
 
     for one in ssq_made:
         one.wait_recv()
     for m in range(2):
         lanes = pl.ds(256 * m, 256)
         total = ssq[0, :, lanes] + ssq[1, :, lanes] + ssq[2, :, lanes] + ssq[3, :, lanes]
-        root[lanes, :] = as_column(jnp.sqrt(total * (1.0 / 4096) + EPS)[0:1, :])
+        root[lanes, :] = as_column((1.0 / jnp.sqrt(total * (1.0 / 4096) + EPS))[0:1, :])
 
     for j in range(4):
         target = lax.rem(x + j, 4)
@@ -224,11 +288,12 @@
         part = gain[:, rows_of(z * 4 + target, 256)]
         kept = nmz.at[0, 0] if j == 0 else nms.at[j - 1]
 
-        @pl.loop(0, 8)
+        @pl.loop(0, 4)
         def _(i):
-            rows = rows_of(i, 64)
-            unit = inp[rows, lanes].astype(F32) / root[rows, 0:1]
-            kept[rows, :] = (unit * part).astype(BF16)
+            rows = rows_of(i, 128)
+            unit = inp[rows, lanes].astype(F32) * root[rows, 0:1]
+            un[rows, lanes] = unit
+            kept[:, rows] = (unit * part).T.astype(BF16)
 
     nx_made = [copy(nms.at[j - 1], nmz.at[0, 4 - j], x_to[j]) for j in (1, 2, 3)]
     for one in nx_made:
@@ -250,10 +315,7 @@
     up_made["fb"].wait_recv()
     take_upstream(2)
 
-    @pl.loop(0, 16)
-    def _(i):
-        rows = rows_of(i, 32)
-        ag[rows, :] = aga[rows, :].astype(BF16)
+    out_mid(0)
 
     qk_made = [
         gather([qk.at[group, r] for r in range(4)], x_to, first, second) for group in range(2)
@@ -281,13 +343,10 @@
 
         gather_start(qk_made[group])
 
+    out_terms(2)
+    out_mid(3)
+    out_mid(1)
     gather_relay(nm_made)
-    out_terms(2)
-    o_made = scatter(
-        o_s.at[lax.rem(y + 2, 4)], o_s.at[lax.rem(y + 1, 4)], o_s.at[lax.rem(y + 3, 4)],
-        256, o_y1, o_y2, y_to,
-    )
-    scatter_start(o_made)
     gather_relay(qk_made[0])
     loads[4].wait()
 
@@ -300,21 +359,25 @@
     ]
 
     def qkv_terms(group):
-        def one(j):
-            block = lax.rem(y + j + 2, 4)
+        for j in (2, 1, 3, 0):
+            block = lax.rem(y + j, 4)
             slot = lax.rem(block - z + 4, 4)
-            term = dot(nmz[slot].reshape(2048, 256), qk[group].reshape(2048, 512), TN)
+            normed = jnp.concatenate([nmz[slot, r] for r in range(4)], axis=1)
+            term = dot(normed, qk[group].reshape(2048, 512), NN)
+            q_y[group, block] = term.astype(BF16)
+            if j == 2:
+                q_made[group]["fa"].start()
+                q_made[group]["fb"].start()
+            elif j == 1:
+                q_made[group]["rb"].start()
+            elif j == 3:
+                q_made[group]["la"].start()
             weight = wq[block, rows_of(x, 256), pl.ds(512 * group, 512)].astype(F32)
             row = as_row(jnp.sum(term * weight, axis=-1, keepdims=True))
             if group == 0:
                 gp[slot] = row
             else:
                 gp[slot] += row
-            q_y[group, block] = term.astype(BF16)
-
-        one(0)
-        scatter_start(q_made[group])
-        pl.loop(1, 4)(one)
 
     z_made = scatter(wo.at[2], wo.at[1], wo.at[3], 256, g_1, g_2, z_to, keep=False)
 
@@ -332,7 +395,7 @@
         scatter_start(z_made)
 
     gather_relay(qk_made[1])
-    scatter_mid(o_made)
+    out_mid(2)
     gather_wait(nm_made)
     gather_wait(qk_made[0])
     qkv_terms(0)
@@ -383,7 +446,7 @@
         grad = (
             wo[0, rows, :].astype(F32) + g_2[0, rows, :].astype(F32) + g_2[1, rows, :].astype(F32)
         )
-        return grad * gain[:, rows_of(z, 1024)], inp[rows, :].astype(F32) / root[rows, 0:1]
+        return grad * gain[:, rows_of(z, 1024)], un[rows, :]
 
     @pl.when(sec == 1)
     def _():
@@ -412,7 +475,8 @@
     for one in gx_made:
         one.start()
 
-    passed_made = copy(layer, passed, other, keep=False)
+    pieces = [pl.ds(128 * i, 128) for i in range(4)]
+    passed_made = [copy(layer.at[piece], passed.at[piece], other, keep=False) for piece in pieces]
 
     @pl.when(sec == 1)
     def _():
@@ -424,22 +488,25 @@
             rtot[lanes, :] = as_column((total * (1.0 / 4096))[0:1, :])
         straight = order[0:1, 0:1] == 0
 
-        @pl.loop(0, 16)
-        def _(i):
-            both = []
-            for m in range(2):
-                rows = pl.ds(pl.multiple_of(m * 256 + i * 16, 16), 16)
-                scaled, unit = scaled_unit(rows)
-                through = up[rows, :].astype(F32) + (scaled - unit * rtot[rows, 0:1]) / root[rows, 0:1]
-                both.append(through)
-            low, high = both
-            keep_order = jnp.broadcast_to(straight, (16, 1024))
-            rows = pl.ds(pl.multiple_of(i * 16, 16), 16)
-            layer[rows, :] = jnp.where(keep_order, low, high).astype(BF16)
-            rows = pl.ds(pl.multiple_of(256 + i * 16, 16), 16)
-            layer[rows, :] = jnp.where(keep_order, high, low).astype(BF16)
-
-        passed_made.start()
+        for half in range(2):
+
+            @pl.loop(8 * half, 8 * half + 8)
+            def _(i):
+                both = []
+                for m in range(2):
+                    rows = pl.ds(pl.multiple_of(m * 256 + i * 16, 16), 16)
+                    scaled, unit = scaled_unit(rows)
+                    through = up[rows, :].astype(F32) + (scaled - unit * rtot[rows, 0:1]) * root[rows, 0:1]
+                    both.append(through)
+                low, high = both
+                keep_order = jnp.broadcast_to(straight, (16, 1024))
+                rows = pl.ds(pl.multiple_of(i * 16, 16), 16)
+                layer[rows, :] = jnp.where(keep_order, low, high).astype(BF16)
+                rows = pl.ds(pl.multiple_of(256 + i * 16, 16), 16)
+                layer[rows, :] = jnp.where(keep_order, high, low).astype(BF16)
+
+            passed_made[half].start()
+            passed_made[half + 2].start()
 
         @pl.loop(0, 16)
         def _(i):
@@ -473,15 +540,28 @@
 
     @pl.when(sec == 0)
     def _():
-        passed_made.wait_recv()
+        for one in passed_made:
+            one.wait_recv()
 
     @pl.when(sec == 1)
     def _():
-        for one in [z_made[name] for name in "abrl"] + row_made + [passed_made]:
+        for one in [z_made[name] for name in SIX] + row_made + passed_made:
             one.wait_send()
 
     for one in sent:
         one.wait_send()
+
+
+def finish(passed, qkv_sum, out_sum, gain_sum, passed_out, qkv_out, out_out, gain_out):
+    @pl.loop(0, 4)
+    def _(i):
+        rows = rows_of(i, 16)
+        low, high = passed[0, rows, :].astype(F32), passed[1, rows, :].astype(F32)
+        passed_out[rows] = jnp.stack([low, high], axis=1).astype(BF16)
+
+    qkv_out[...] = qkv_sum[...]
+    out_out[...] = out_sum[...]
+    gain_out[...] = gain_sum[0:1, :]
 
 
 def shards(
@@ -496,9 +576,6 @@
     qkv_weight,
     out_weight,
 ):
-    def by_micro(array):
-        return array[0].transpose(1, 0, 2).reshape(512, array.shape[3])
-
     vmem = pl.BlockSpec(memory_space=pltpu.VMEM)
     hbm = pl.BlockSpec(memory_space=pl.ANY)
     passed, qkv_grad, out_grad, gain_grad = pl.pallas_call(
@@ -509,12 +586,12 @@
             jax.ShapeDtypeStruct((512, 256), F32),
             jax.ShapeDtypeStruct((8, 1024), F32),
         ),
-        in_specs=[vmem] * 8 + [hbm] * 2,
+        in_specs=[hbm] * 5 + [vmem] * 3 + [hbm] * 2,
         out_specs=(vmem,) * 4,
         scratch_shapes=[
             pltpu.VMEM((3, 512, 1024), BF16),
-            pltpu.VMEM((3, 512, 256), BF16),
-            pltpu.VMEM((4, 4, 512, 256), BF16),
+            pltpu.VMEM((3, 256, 512), BF16),
+            pltpu.VMEM((4, 4, 256, 512), BF16),
             pltpu.VMEM((4, 512, 1024), BF16),
             pltpu.VMEM((4, 1024, 1024), BF16),
             pltpu.VMEM((8, 256, 256), F32),
@@ -542,27 +619,59 @@
             pltpu.VMEM((3, 8, 256), F32),
             pltpu.VMEM((4, 8, 256), F32),
             pltpu.VMEM((4, 8, 256), F32),
-            pltpu.SemaphoreType.DMA((5,)),
-            pltpu.SemaphoreType.DMA((80,)),
-            pltpu.SemaphoreType.DMA((80,)),
+            pltpu.VMEM((256, 2, 1024), BF16),
+            pltpu.VMEM((256, 2, 1024), BF16),
+            pltpu.VMEM((256, 2, 512), BF16),
+            pltpu.VMEM((256, 2, 256), BF16),
+            pltpu.VMEM((256, 2, 256), BF16),
+            pltpu.VMEM((512, 1024), BF16),
+            pltpu.VMEM((512, 1024), BF16),
+            pltpu.VMEM((512, 512), BF16),
+            pltpu.VMEM((512, 256), BF16),
+            pltpu.VMEM((512, 256), BF16),
+            pltpu.VMEM((512, 1024), F32),
+            pltpu.SemaphoreType.DMA((10,)),
+            pltpu.SemaphoreType.DMA((90,)),
+            pltpu.SemaphoreType.DMA((90,)),
         ],
         compiler_params=pltpu.CompilerParams(
             collective_id=0, has_side_effects=True, vmem_limit_bytes=67043328
         ),
     )(
-        by_micro(upstream_grad),
-        by_micro(layer_input),
-        by_micro(saved_queries),
-        by_micro(saved_keys),
-        by_micro(saved_values),
+        upstream_grad[0],
+        layer_input[0],
+        saved_queries[0],
+        saved_keys[0],
+        saved_values[0],
         segment_ids[0],
         norm_gain,
         batch_order[0],
         qkv_weight[0].reshape(4, 1024, 1024),
         out_weight[0],
     )
-    passed = passed.reshape(2, 256, 1024).transpose(1, 0, 2)
-    return (passed[None], qkv_grad[None], out_grad[None], gain_grad[0:1])
+    passed, qkv_grad, out_grad, gain_grad = pl.pallas_call(
+        finish,
+        grid=(4,),
+        out_shape=(
+            jax.ShapeDtypeStruct((256, 2, 1024), BF16),
+            jax.ShapeDtypeStruct((256, 1024), F32),
+            jax.ShapeDtypeStruct((512, 256), F32),
+            jax.ShapeDtypeStruct((1, 1024), F32),
+        ),
+        in_specs=[
+            pl.BlockSpec((2, 64, 1024), lambda i: (0, i, 0)),
+            pl.BlockSpec((64, 1024), lambda i: (i, 0)),
+            pl.BlockSpec((128, 256), lambda i: (i, 0)),
+            pl.BlockSpec((8, 1024), lambda i: (0, 0)),
+        ],
+        out_specs=(
+            pl.BlockSpec((64, 2, 1024), lambda i: (i, 0, 0)),
+            pl.BlockSpec((64, 1024), lambda i: (i, 0)),
+            pl.BlockSpec((128, 256), lambda i: (i, 0)),
+            pl.BlockSpec((1, 1024), lambda i: (0, 0)),
+        ),
+    )(passed.reshape(2, 256, 1024), qkv_grad, out_grad, gain_grad)
+    return (passed[None], qkv_grad[None], out_grad[None], gain_grad)
 
 
 def solution(mesh):

time: 139 us -> 114 us (0.82)
  local copies, waits for them, and re-layouts: 19 us -> 0 us
  Pallas kernels: 118 us -> 112 us
    pallas_call x1, Pallas kernels: 118 us -> 107 us  [shards(): pl.pallas_call(kernel, out_shape=(jax.ShapeDtypeStruct((512, 1024), BF16)...]
    transpose x5 -> x0, local copies, waits for them, and re-layouts: 10.2 us -> none  [by_micro(): return array[0].transpose(1, 0, 2).reshape(512, array.shape[3])]
    pallas_call x0 -> x1, Pallas kernels: none -> 4.78 us  [shards(): pl.pallas_call(finish, grid=(4,), out_shape=(jax.ShapeDtypeStruct((256, 2...]
    unnamed x2 -> x0, local copies, waits for them, and re-layouts: 4.17 us -> none
    reshape x1 -> x0, local copies, waits for them, and re-layouts: 3.27 us -> none  [shards(): passed = passed.reshape(2, 256, 1024).transpose(1, 0, 2)]
where the time goes in v3:
time: 114 us; the launch traced here: 113 us
  Pallas kernels  112 us (98%)
    pallas_call x1, Pallas kernels, shards(): pl.pallas_call(kernel, out_shape=(jax.ShapeDtypeStruct((512, 1024), BF16)...  107 us
    pallas_call x1, Pallas kernels, shards(): pl.pallas_call(finish, grid=(4,), out_shape=(jax.ShapeDtypeStruct((256, 2...  4.78 us

profile of v3, /device:TPU:0, one launch (start us, length us, event | category | flops | bytes accessed | tf_op | source)
XLA Modules:
  0.0 112.8 jit_solution(1252831113700388961)
XLA Ops:
  0.6 107.3 %shard_map.129 = (bf16[512,1024]{1,0:T(8,128)(2,1)}, f32[256,1024]{1,0:T(8,128)}, f32[512,256]{1,0:T(8,128)}, f32[8,1024]{1,0:T(8,128)}) custom-call(bf16[256,2,1024]{2,1,0:T(2,128)(2,1)} %bitcast.15, bf16[256,2,1024]{2,1,0:T(2,128)(2,1)} %bitcast.16, bf16[256,2,512]{2,1,0:T(2,128)(2,1)} %bitcast.18, bf16[256,2,256]{2,1,0:T(2,128)(2,1)} %bitcast.19, ...), custom_call_target="tpu_custom_call" | custom-call | tf_op jit(solution)/shard_map/pallas_call | solution.py:581
  108.0 4.8 %shard_map.130 = (bf16[256,2,1024]{2,1,0:T(2,128)(2,1)}, f32[256,1024]{1,0:T(8,128)}, f32[512,256]{1,0:T(8,128)}, f32[1,1024]{1,0:T(1,128)}) custom-call(bf16[2,256,1024]{2,1,0:T(8,128)(2,1)} %bitcast.17, f32[256,1024]{1,0:T(8,128)} %get-tuple-element.13.qkv_sum, f32[512,256]{1,0:T(8,128)} %get-tuple-element.14.out_sum, f32[8,1024]{1,0:T(8,128)} %get-tuple-element.15.gain_sum), custom_call_target="tpu_custom_call" | custom-call | tf_op jit(solution)/shard_map/pallas_call | solution.py:652

commit v4 on v3

--- a/solution.py
+++ b/solution.py
@@ -39,7 +39,7 @@
 def kernel(
     up_hbm, inp_hbm, q_hbm, k_hbm, v_hbm, seg, gain, order, wq_hbm, wo_hbm,
     passed, qg, og, gg,
-    upb, nms, nmz, wo, wq, probs, ao, aga, ag, qk,
+    upb, nms, nmz, wo, wq, probs, ao, aga, wide, qk,
     o_s, o_y1, o_y2, o_x, o_x1, o_x2,
     q_y, q_y1, q_y2,
     g_1, g_2, ssq, rowp, root, rtot, segc, gp, gz, gy, gx,
@@ -87,6 +87,14 @@
     for one in fetches + loads:
         one.start()
 
+    def as_rows(which):
+        fetches[which].wait()
+        _, raw, kept = stored[which]
+
+        @pl.loop(0, 16)
+        def _(i):
+            kept[rows_of(i, 32), :] = raw[rows_of(i, 16)].reshape(32, 1024)
+
     def by_micro(which):
         fetches[which].wait()
         _, raw, kept = stored[which]
@@ -172,16 +180,16 @@
 
     up_slots = [up, upb.at[0], upb.at[1], upb.at[2]]
     up_made = gather(up_slots, z_to, first, second)
-    by_micro(0)
+    as_rows(0)
     up_made["ra"].start()
     up_made["lb"].start()
-    by_micro(1)
+    as_rows(1)
 
     for m in range(2):
         total = jnp.zeros((256, 1), F32)
         for c in range(4):
-            wide = inp[pl.ds(256 * m, 256), pl.ds(256 * c, 256)].astype(F32)
-            total += jnp.sum(wide * wide, axis=-1, keepdims=True)
+            part = inp[pl.ds(256 * m, 256), pl.ds(256 * c, 256)].astype(F32)
+            total += jnp.sum(part * part, axis=-1, keepdims=True)
         ssq[0, :, pl.ds(256 * m, 256)] = as_row(total)
     ssq_made = [copy(ssq.at[0], ssq.at[s], z_to[s]) for s in (1, 2, 3)]
     for one in ssq_made:
@@ -211,7 +219,11 @@
         shifted = jnp.where(visible, jnp.exp(scores - top), 0.0)
         weights = shifted / jnp.sum(shifted, axis=-1, keepdims=True)
         probs[i] = weights
-        ao[rows_of(head, 128), rows] = dot(weights.astype(BF16), v[rows, lanes], NN).T.astype(BF16)
+        wide[head, pl.ds(m, 256, stride=2), :] = dot(weights.astype(BF16), v[rows, lanes], NN)
+
+    @pl.loop(0, 4)
+    def _(i):
+        ao[rows_of(i, 128), :] = wide[i].T.astype(BF16)
 
     for one in loads[:4]:
         one.wait()
@@ -224,12 +236,9 @@
         def _(m):
             rows = rows_of(m, 256)
             term = dot(ref[rows, :], wo[block], NT)
-            if slot == 0:
-                aga[rows, :] = term
-            elif slot == 2:
-                ag[rows, :] = (aga[rows, :] + term).astype(BF16)
-            else:
-                aga[rows, :] += term
+            for c in range(4):
+                part = term[:, 128 * c : 128 * c + 128]
+                aga[c, rows, :] = part if slot == 0 else aga[c, rows, :] + part
 
     o_made = scatter(
         o_s.at[lax.rem(y + 2, 4)], o_s.at[lax.rem(y + 1, 4)], o_s.at[lax.rem(y + 3, 4)],
@@ -326,28 +335,37 @@
         @pl.loop(0, 2)
         def _(m):
             rows = rows_of(m, 256)
+            mine = pl.ds(m, 256, stride=2)
             key_grad = jnp.zeros((256, 128), F32)
             value_grad = jnp.zeros((256, 128), F32)
             for h in range(2):
                 head = pl.ds(128 * (group * 2 + h), 128)
-                grad = ag[rows, head]
+                grad = aga[group * 2 + h, mine, :].astype(BF16)
                 weights = probs[m * 4 + group * 2 + h]
                 probs_grad = dot(grad, v[rows, lanes], NT)
                 row_dot = jnp.sum(weights * probs_grad, axis=-1, keepdims=True)
                 score_grad = (weights * (probs_grad - row_dot) * SCALE).astype(BF16)
-                qk[group, 0, rows, pl.ds(128 * h, 128)] = dot(score_grad, k[rows, lanes], NN).astype(BF16)
+                wide[h, mine, :] = dot(score_grad, k[rows, lanes], NN)
                 key_grad += dot(score_grad, q[rows, head], TN)
                 value_grad += dot(weights.astype(BF16), grad, TN)
-            qk[group, 0, rows, pl.ds(256, 128)] = key_grad.astype(BF16)
-            qk[group, 0, rows, pl.ds(384, 128)] = value_grad.astype(BF16)
-
-        gather_start(qk_made[group])
+            wide[2, mine, :] = key_grad
+            wide[3, mine, :] = value_grad
+
+        @pl.loop(0, 8)
+        def _(i):
+            rows = rows_of(i, 64)
+            for c in range(4):
+                qk[group, 0, rows, pl.ds(128 * c, 128)] = wide[c, rows, :].astype(BF16)
+
+        if group == 0:
+            gather_start(qk_made[0])
 
     out_terms(2)
     out_mid(3)
     out_mid(1)
+    gather_relay(qk_made[0])
+    gather_start(qk_made[1])
     gather_relay(nm_made)
-    gather_relay(qk_made[0])
     loads[4].wait()
 
     q_made = [
@@ -358,26 +376,44 @@
         for group in range(2)
     ]
 
-    def qkv_terms(group):
-        for j in (2, 1, 3, 0):
-            block = lax.rem(y + j, 4)
-            slot = lax.rem(block - z + 4, 4)
-            normed = jnp.concatenate([nmz[slot, r] for r in range(4)], axis=1)
-            term = dot(normed, qk[group].reshape(2048, 512), NN)
-            q_y[group, block] = term.astype(BF16)
-            if j == 2:
-                q_made[group]["fa"].start()
-                q_made[group]["fb"].start()
-            elif j == 1:
-                q_made[group]["rb"].start()
-            elif j == 3:
-                q_made[group]["la"].start()
-            weight = wq[block, rows_of(x, 256), pl.ds(512 * group, 512)].astype(F32)
-            row = as_row(jnp.sum(term * weight, axis=-1, keepdims=True))
-            if group == 0:
-                gp[slot] = row
-            else:
-                gp[slot] += row
+    def qkv_terms(group, slot):
+        block = lax.rem(z + slot, 4)
+        role = lax.rem(block - y + 4, 4)
+        made = q_made[group]
+        normed = jnp.concatenate([nmz[slot, r] for r in range(4)], axis=1)
+        term = dot(normed, qk[group].reshape(2048, 512), NN)
+        q_y[group, block] = term.astype(BF16)
+
+        @pl.when(role == 2)
+        def _():
+            made["fa"].start()
+            made["fb"].start()
+
+        @pl.when(role == 1)
+        def _():
+            made["rb"].start()
+
+        @pl.when(role == 3)
+        def _():
+            made["la"].start()
+
+        weight = wq[block, rows_of(x, 256), pl.ds(512 * group, 512)].astype(F32)
+        row = as_row(jnp.sum(term * weight, axis=-1, keepdims=True))
+        if group == 0:
+            gp[slot] = row
+        else:
+            gp[slot] += row
+
+    def qkv_mid(group, slot):
+        role = lax.rem(lax.rem(z + slot, 4) - y + 4, 4)
+
+        @pl.when(role == 1)
+        def _():
+            scatter_mid_a(q_made[group])
+
+        @pl.when(role == 3)
+        def _():
+            scatter_mid_b(q_made[group])
 
     z_made = scatter(wo.at[2], wo.at[1], wo.at[3], 256, g_1, g_2, z_to, keep=False)
 
@@ -394,18 +430,30 @@
 
         scatter_start(z_made)
 
+    gather_wait(qk_made[0])
+    qkv_terms(0, 0)
+    nm_made["rb"].wait_recv()
+    qkv_terms(0, 3)
+    nm_made["la"].wait_recv()
+    qkv_terms(0, 1)
+    out_mid(2)
     gather_relay(qk_made[1])
-    out_mid(2)
-    gather_wait(nm_made)
-    gather_wait(qk_made[0])
-    qkv_terms(0)
+    qkv_mid(0, 0)
+    nm_made["fa"].wait_recv()
+    nm_made["fb"].wait_recv()
+    qkv_terms(0, 2)
+    qkv_mid(0, 3)
+    qkv_mid(0, 1)
 
     @pl.when(sec == 1)
     def _():
         scatter_mid(z_made)
 
     gather_wait(qk_made[1])
-    qkv_terms(1)
+    for slot in (0, 3, 1, 2):
+        qkv_terms(1, slot)
+
+    qkv_mid(0, 2)
 
     gz_made = [copy(gp.at[r], gz.at[r - 1], z_to[r]) for r in (1, 2, 3)]
     for one in gz_made:
@@ -430,7 +478,9 @@
 
     ox_made = scatter(o_x.at[2], o_x.at[1], o_x.at[3], 256, o_x1, o_x2, x_to)
     scatter_start(ox_made)
-    scatter_mid(q_made[0])
+    qkv_mid(1, 0)
+    qkv_mid(1, 3)
+    qkv_mid(1, 1)
 
     for one in gz_made:
         one.wait_recv()
@@ -465,8 +515,8 @@
         for one in row_made:
             one.start()
 
+    qkv_mid(1, 2)
     scatter_mid(ox_made)
-    scatter_mid(q_made[1])
 
     for one in gy_made:
         one.wait_recv()
@@ -488,25 +538,21 @@
             rtot[lanes, :] = as_column((total * (1.0 / 4096))[0:1, :])
         straight = order[0:1, 0:1] == 0
 
-        for half in range(2):
-
-            @pl.loop(8 * half, 8 * half + 8)
+        even = lax.rem(lax.broadcasted_iota(jnp.int32, (4, 8, 1024), 1), 2) == 0
+        keep_order = jnp.broadcast_to(straight, (4, 8, 1024))
+        for piece in range(4):
+
+            @pl.loop(4 * piece, 4 * piece + 4)
             def _(i):
-                both = []
-                for m in range(2):
-                    rows = pl.ds(pl.multiple_of(m * 256 + i * 16, 16), 16)
-                    scaled, unit = scaled_unit(rows)
-                    through = up[rows, :].astype(F32) + (scaled - unit * rtot[rows, 0:1]) * root[rows, 0:1]
-                    both.append(through)
-                low, high = both
-                keep_order = jnp.broadcast_to(straight, (16, 1024))
-                rows = pl.ds(pl.multiple_of(i * 16, 16), 16)
-                layer[rows, :] = jnp.where(keep_order, low, high).astype(BF16)
-                rows = pl.ds(pl.multiple_of(256 + i * 16, 16), 16)
-                layer[rows, :] = jnp.where(keep_order, high, low).astype(BF16)
-
-            passed_made[half].start()
-            passed_made[half + 2].start()
+                rows = rows_of(i, 32)
+                scaled, unit = scaled_unit(rows)
+                through = up[rows, :].astype(F32) + (scaled - unit * rtot[rows, 0:1]) * root[rows, 0:1]
+                through = through.reshape(4, 8, 1024)
+                swapped = jnp.where(even, pltpu.roll(through, 7, 1), pltpu.roll(through, 1, 1))
+                picked = jnp.where(keep_order, through, swapped)
+                layer[rows, :] = picked.reshape(32, 1024).astype(BF16)
+
+            passed_made[piece].start()
 
         @pl.loop(0, 16)
         def _(i):
@@ -553,12 +599,7 @@
 
 
 def finish(passed, qkv_sum, out_sum, gain_sum, passed_out, qkv_out, out_out, gain_out):
-    @pl.loop(0, 4)
-    def _(i):
-        rows = rows_of(i, 16)
-        low, high = passed[0, rows, :].astype(F32), passed[1, rows, :].astype(F32)
-        passed_out[rows] = jnp.stack([low, high], axis=1).astype(BF16)
-
+    passed_out[...] = passed[...].reshape(64, 2, 1024)
     qkv_out[...] = qkv_sum[...]
     out_out[...] = out_sum[...]
     gain_out[...] = gain_sum[0:1, :]
@@ -596,8 +637,8 @@
             pltpu.VMEM((4, 1024, 1024), BF16),
             pltpu.VMEM((8, 256, 256), F32),
             pltpu.VMEM((512, 512), BF16),
-            pltpu.VMEM((512, 512), F32),
-            pltpu.VMEM((512, 512), BF16),
+            pltpu.VMEM((4, 512, 128), F32),
+            pltpu.VMEM((4, 512, 128), F32),
             pltpu.VMEM((2, 4, 512, 512), BF16),
             pltpu.VMEM((4, 512, 1024), BF16),
             pltpu.VMEM((2, 256, 1024), BF16),
@@ -659,7 +700,7 @@
             jax.ShapeDtypeStruct((1, 1024), F32),
         ),
         in_specs=[
-            pl.BlockSpec((2, 64, 1024), lambda i: (0, i, 0)),
+            pl.BlockSpec((128, 1024), lambda i: (i, 0)),
             pl.BlockSpec((64, 1024), lambda i: (i, 0)),
             pl.BlockSpec((128, 256), lambda i: (i, 0)),
             pl.BlockSpec((8, 1024), lambda i: (0, 0)),
@@ -670,7 +711,7 @@
             pl.BlockSpec((128, 256), lambda i: (i, 0)),
             pl.BlockSpec((1, 1024), lambda i: (0, 0)),
         ),
-    )(passed.reshape(2, 256, 1024), qkv_grad, out_grad, gain_grad)
+    )(passed, qkv_grad, out_grad, gain_grad)
     return (passed[None], qkv_grad[None], out_grad[None], gain_grad)
 
 

time: 114 us -> 111 us (0.974)
  Pallas kernels: 112 us -> 109 us
    pallas_call x1, Pallas kernels: 107 us -> 105 us  [shards(): pl.pallas_call(kernel, out_shape=(jax.ShapeDtypeStruct((512, 1024), BF16)...]
where the time goes in v4:
time: 111 us; the launch traced here: 110 us
  Pallas kernels  109 us (98%)
    pallas_call x1, Pallas kernels, shards(): pl.pallas_call(kernel, out_shape=(jax.ShapeDtypeStruct((512, 1024), BF16)...  105 us
    pallas_call x1, Pallas kernels, shards(): pl.pallas_call(finish, grid=(4,), out_shape=(jax.ShapeDtypeStruct((256, 2...  4.01 us

profile of v4, /device:TPU:0, one launch (start us, length us, event | category | flops | bytes accessed | tf_op | source)
XLA Modules:
  0.0 109.6 jit_solution(5180165562270647449)
XLA Ops:
  0.6 104.9 %shard_map.129 = (bf16[512,1024]{1,0:T(8,128)(2,1)}, f32[256,1024]{1,0:T(8,128)}, f32[512,256]{1,0:T(8,128)}, f32[8,1024]{1,0:T(8,128)}) custom-call(bf16[256,2,1024]{2,1,0:T(2,128)(2,1)} %bitcast.14, bf16[256,2,1024]{2,1,0:T(2,128)(2,1)} %bitcast.15, bf16[256,2,512]{2,1,0:T(2,128)(2,1)} %bitcast.16, bf16[256,2,256]{2,1,0:T(2,128)(2,1)} %bitcast.17, ...), custom_call_target="tpu_custom_call" | custom-call | tf_op jit(solution)/shard_map/pallas_call | solution.py:622
  105.6 4.0 %shard_map.130 = (bf16[256,2,1024]{2,1,0:T(2,128)(2,1)}, f32[256,1024]{1,0:T(8,128)}, f32[512,256]{1,0:T(8,128)}, f32[1,1024]{1,0:T(1,128)}) custom-call(bf16[512,1024]{1,0:T(8,128)(2,1)} %get-tuple-element.12.passed, f32[256,1024]{1,0:T(8,128)} %get-tuple-element.13.qkv_sum, f32[512,256]{1,0:T(8,128)} %get-tuple-element.14.out_sum, ...), custom_call_target="tpu_custom_call" | custom-call | tf_op jit(solution)/shard_map/pallas_call | solution.py:693
